TPU v7x, 32 devices: a whole 2x2x4 slice. The times are simulated.
32 devices in a mesh: hst: 2 (over core), row: 4 (over y, x), col: 4 (over z).
Axes of the slice: x: 2, y: 2, z: 4, core: 2. Of those that a mesh axis runs over, the one named last changes fastest.
Arguments:
- tables: bfloat16 [256, 1024, 128], P(('hst', 'row', 'col')), may hold values from -6 to 6
- indices: int32 [256, 512, 4], P(('hst', 'row', 'col')), may hold values from 0 to 1023
- lengths: int32 [256, 512], P(('hst', 'row', 'col')), may hold values from 1 to 4, as said below
- table_slot: int32 [256], replicated, may hold values from 0 to 255, each once
- dense_feature: bfloat16 [512, 128], P(('hst', 'row', 'col')), may hold values from -48 to 48
- left_proj: bfloat16 [128, 257], replicated, may hold values from -0.375 to 0.375
- right_proj: bfloat16 [128, 257], replicated, may hold values from -0.375 to 0.375
Outputs:
- interaction: bfloat16 [512, 16384], P(('hst', 'row', 'col'))
Inputs may be any that keep to these rules, and one draw needn't show every extreme that they name: Each bag uses its first lengths ids; some bag holds 4 ids.
All inputs are finite; a program needn't handle non-finite values.
Results may differ from a plain program's by a relative error of at most 0.0063.
Values may be sent and summed in bfloat16 or wider, within the bound.
No kernel may reach another device: no remote copies, remote signals or barrier semaphores. Data moves between devices by JAX's collectives and lax.ppermute only.
A program may use at most 64 MiB of HBM per device.

v0:
```python
import jax
import jax.numpy as jnp
from jax import lax
from jax.sharding import PartitionSpec as P


def pool_table(table, row_ids, bag_lens, bag_size):
    all_samples = row_ids.shape[0]
    table_rows = table.shape[0]
    feature_width = table.shape[1]
    block = 512
    row_iota = lax.broadcasted_iota(jnp.int32, (1, table_rows), 1)

    def one_block(items):
        block_ids, block_lens = items

        def add_ids(position, counts):
            chosen_ids = lax.dynamic_index_in_dim(block_ids, position, 1, keepdims=False)
            hit = (chosen_ids[:, None] == row_iota) & (position < block_lens)[:, None]
            return counts + hit.astype(jnp.bfloat16)

        counts = jnp.zeros((block, table_rows), jnp.bfloat16)
        counts = lax.fori_loop(0, bag_size, add_ids, counts)
        return jnp.dot(counts, table, preferred_element_type=jnp.float32).astype(jnp.bfloat16)

    grouped_ids = row_ids.reshape(all_samples // block, block, row_ids.shape[1])
    grouped_lens = bag_lens.reshape(all_samples // block, block)
    pooled = lax.map(one_block, (grouped_ids, grouped_lens))
    return pooled.reshape(all_samples, feature_width)


def shards(tables, indices, lengths, table_slot, dense_feature, left_proj, right_proj):
    tab_dev, all_samples, bag_size = indices.shape
    feature_width = tables.shape[2]
    devices = lax.axis_size(("hst", "row", "col"))
    own_samples = all_samples // devices
    proj_rows = left_proj.shape[0]
    tables_total = left_proj.shape[1] - 1
    pooled = lax.map(
        lambda items: pool_table(items[0], items[1], items[2], bag_size), (tables, indices, lengths)
    )
    blocks = pooled.reshape(tab_dev, devices, own_samples, feature_width)
    positions = jnp.arange(tables_total, dtype=jnp.int32)
    within = positions % tab_dev
    source = positions // tab_dev
    slot_here = source * tab_dev + within
    projections = jnp.concatenate([left_proj, right_proj], axis=0)
    selector = (table_slot[:, None] == slot_here[None, :]).astype(jnp.bfloat16)
    proj_here = jnp.dot(projections[:, 1:], selector, preferred_element_type=jnp.float32).astype(
        jnp.bfloat16
    )
    received = lax.all_to_all(
        blocks, ("hst", "row", "col"), split_axis=1, concat_axis=0, tiled=True
    )
    count = received.shape[2]
    flattened = received.reshape(tables_total, count * feature_width)
    mixed_all = jnp.dot(proj_here, flattened, preferred_element_type=jnp.float32)
    mixed_all = mixed_all.reshape(2 * proj_rows, count, feature_width)
    dense_column = projections[:, 0].astype(jnp.float32)
    mixed_all = mixed_all + dense_column[:, None, None] * dense_feature[None].astype(jnp.float32)
    mixed_all = mixed_all.astype(jnp.bfloat16)
    left_side = mixed_all[:proj_rows]
    right_side = mixed_all[proj_rows:]
    products = jnp.einsum("kbe,lbe->bkl", left_side, right_side, preferred_element_type=jnp.float32)
    products = products * (1.0 / feature_width)
    return products.reshape(own_samples, proj_rows * proj_rows).astype(jnp.bfloat16)


def solution(mesh):
    in_specs = (
        P(("hst", "row", "col"), None, None),
        P(("hst", "row", "col"), None, None),
        P(("hst", "row", "col"), None),
        P(),
        P(("hst", "row", "col"), None),
        P(),
        P(),
    )
    out_specs = P(("hst", "row", "col"), None)
    return jax.shard_map(shards, mesh=mesh, in_specs=in_specs, out_specs=out_specs, check_vma=False)
```

profile of v0, /device:TPU:0, one launch (start us, length us, event | category | flops | bytes accessed | tf_op | source)
XLA Modules:
  0.0 83.0 jit_solution(462694568303462311)
XLA Ops:
  0.0 44.5 %while.32 = (s32[]{:T(128)}, bf16[8,512,128]{2,1,0:T(8,128)(2,1)S(1)}, s32[8,512,4]{1,2,0:T(4,128)}, s32[8,512]{1,0:T(8,128)}, bf16[8,1024,128]{2,1,0:T(8,128)(2...) while((s32[]{:T(128)}, bf16[8,512,128]{2,1,0:T(8,128)(2,1)S(1)}, s32[8,512,4]{1,2,0:T(4,128)}, ...), condition=%wide.region_3.4_spmd, body=%wide.region_0.3_spmd.sunk | while | flops 138478080 | bytes 3569924 | solution.py:39
  0.7 0.7 constant_dynamic-slice_fusion.4
  1.4 2.7 %while.33 = (s32[]{:T(128)}, bf16[512,1024]{1,0:T(8,128)(2,1)S(1)}, s32[512,4]{0,1:T(4,128)S(1)}, s32[512]{0:T(512)S(1)}, s32[]{:T(128)}, /*index=5*/s32[]{:T(128)}) while((s32[]{:T(128)}, bf16[512,1024]{1,0:T(8,128)(2,1)S(1)}, s32[512,4]{0,1:T(4,128)S(1)}, s32[512]{0:T(512)S(1)}, s32[]{:T(128)}, /*index=5*/s32[]{:T(128)}) %tuple.57), condition=%wide.region_2.2_spmd.clone, body=%wide.region_1.1_spmd.clone.sunk | while | flops 4194819 | bytes 2106463 | solution.py:23
  4.1 1.4 %fusion.34 = bf16[8,512,128]{2,1,0:T(8,128)(2,1)S(1)} fusion(bf16[8,512,128]{2,1,0:T(8,128)(2,1)S(1)} %get-tuple-element.282, s32[]{:T(128)S(6)} %copy.26, bf16[512,1024]{1,0:T(8,128)(2,1)S(1)} %get-tuple-element.248, bf16[8,1024,128]{2,1,0:T(8,128)(2,1)} %get-tuple-element.294), kind=kOutput, calls=%fused_computation.9.clone.1 | convolution fusion | flops 134283264 | bytes 1442816 | tf_op jit(solution)/shard_map/while/body/eval_jaxpr/while/body/eval_jaxpr/dot_general | solution.py:24
  6.3 0.7 constant_dynamic-slice_fusion.4
  7.0 2.7 %while.33 = (s32[]{:T(128)}, bf16[512,1024]{1,0:T(8,128)(2,1)S(1)}, s32[512,4]{0,1:T(4,128)S(1)}, s32[512]{0:T(512)S(1)}, s32[]{:T(128)}, /*index=5*/s32[]{:T(128)}) while((s32[]{:T(128)}, bf16[512,1024]{1,0:T(8,128)(2,1)S(1)}, s32[512,4]{0,1:T(4,128)S(1)}, s32[512]{0:T(512)S(1)}, s32[]{:T(128)}, /*index=5*/s32[]{:T(128)}) %tuple.57), condition=%wide.region_2.2_spmd.clone, body=%wide.region_1.1_spmd.clone.sunk | while | flops 4194819 | bytes 2106463 | solution.py:23
  9.6 1.4 %fusion.34 = bf16[8,512,128]{2,1,0:T(8,128)(2,1)S(1)} fusion(bf16[8,512,128]{2,1,0:T(8,128)(2,1)S(1)} %get-tuple-element.282, s32[]{:T(128)S(6)} %copy.26, bf16[512,1024]{1,0:T(8,128)(2,1)S(1)} %get-tuple-element.248, bf16[8,1024,128]{2,1,0:T(8,128)(2,1)} %get-tuple-element.294), kind=kOutput, calls=%fused_computation.9.clone.1 | convolution fusion | flops 134283264 | bytes 1442816 | tf_op jit(solution)/shard_map/while/body/eval_jaxpr/while/body/eval_jaxpr/dot_general | solution.py:24
  12.5 2.7 %while.33 = (s32[]{:T(128)}, bf16[512,1024]{1,0:T(8,128)(2,1)S(1)}, s32[512,4]{0,1:T(4,128)S(1)}, s32[512]{0:T(512)S(1)}, s32[]{:T(128)}, /*index=5*/s32[]{:T(128)}) while((s32[]{:T(128)}, bf16[512,1024]{1,0:T(8,128)(2,1)S(1)}, s32[512,4]{0,1:T(4,128)S(1)}, s32[512]{0:T(512)S(1)}, s32[]{:T(128)}, /*index=5*/s32[]{:T(128)}) %tuple.57), condition=%wide.region_2.2_spmd.clone, body=%wide.region_1.1_spmd.clone.sunk | while | flops 4194819 | bytes 2106463 | solution.py:23
  15.2 1.4 %fusion.34 = bf16[8,512,128]{2,1,0:T(8,128)(2,1)S(1)} fusion(bf16[8,512,128]{2,1,0:T(8,128)(2,1)S(1)} %get-tuple-element.282, s32[]{:T(128)S(6)} %copy.26, bf16[512,1024]{1,0:T(8,128)(2,1)S(1)} %get-tuple-element.248, bf16[8,1024,128]{2,1,0:T(8,128)(2,1)} %get-tuple-element.294), kind=kOutput, calls=%fused_computation.9.clone.1 | convolution fusion | flops 134283264 | bytes 1442816 | tf_op jit(solution)/shard_map/while/body/eval_jaxpr/while/body/eval_jaxpr/dot_general | solution.py:24
  18.1 2.7 %while.33 = (s32[]{:T(128)}, bf16[512,1024]{1,0:T(8,128)(2,1)S(1)}, s32[512,4]{0,1:T(4,128)S(1)}, s32[512]{0:T(512)S(1)}, s32[]{:T(128)}, /*index=5*/s32[]{:T(128)}) while((s32[]{:T(128)}, bf16[512,1024]{1,0:T(8,128)(2,1)S(1)}, s32[512,4]{0,1:T(4,128)S(1)}, s32[512]{0:T(512)S(1)}, s32[]{:T(128)}, /*index=5*/s32[]{:T(128)}) %tuple.57), condition=%wide.region_2.2_spmd.clone, body=%wide.region_1.1_spmd.clone.sunk | while | flops 4194819 | bytes 2106463 | solution.py:23
  20.8 1.4 %fusion.34 = bf16[8,512,128]{2,1,0:T(8,128)(2,1)S(1)} fusion(bf16[8,512,128]{2,1,0:T(8,128)(2,1)S(1)} %get-tuple-element.282, s32[]{:T(128)S(6)} %copy.26, bf16[512,1024]{1,0:T(8,128)(2,1)S(1)} %get-tuple-element.248, bf16[8,1024,128]{2,1,0:T(8,128)(2,1)} %get-tuple-element.294), kind=kOutput, calls=%fused_computation.9.clone.1 | convolution fusion | flops 134283264 | bytes 1442816 | tf_op jit(solution)/shard_map/while/body/eval_jaxpr/while/body/eval_jaxpr/dot_general | solution.py:24
  23.7 2.7 %while.33 = (s32[]{:T(128)}, bf16[512,1024]{1,0:T(8,128)(2,1)S(1)}, s32[512,4]{0,1:T(4,128)S(1)}, s32[512]{0:T(512)S(1)}, s32[]{:T(128)}, /*index=5*/s32[]{:T(128)}) while((s32[]{:T(128)}, bf16[512,1024]{1,0:T(8,128)(2,1)S(1)}, s32[512,4]{0,1:T(4,128)S(1)}, s32[512]{0:T(512)S(1)}, s32[]{:T(128)}, /*index=5*/s32[]{:T(128)}) %tuple.57), condition=%wide.region_2.2_spmd.clone, body=%wide.region_1.1_spmd.clone.sunk | while | flops 4194819 | bytes 2106463 | solution.py:23
  26.3 1.4 %fusion.34 = bf16[8,512,128]{2,1,0:T(8,128)(2,1)S(1)} fusion(bf16[8,512,128]{2,1,0:T(8,128)(2,1)S(1)} %get-tuple-element.282, s32[]{:T(128)S(6)} %copy.26, bf16[512,1024]{1,0:T(8,128)(2,1)S(1)} %get-tuple-element.248, bf16[8,1024,128]{2,1,0:T(8,128)(2,1)} %get-tuple-element.294), kind=kOutput, calls=%fused_computation.9.clone.1 | convolution fusion | flops 134283264 | bytes 1442816 | tf_op jit(solution)/shard_map/while/body/eval_jaxpr/while/body/eval_jaxpr/dot_general | solution.py:24
  28.5 0.7 constant_dynamic-slice_fusion.4
  29.2 2.7 %while.33 = (s32[]{:T(128)}, bf16[512,1024]{1,0:T(8,128)(2,1)S(1)}, s32[512,4]{0,1:T(4,128)S(1)}, s32[512]{0:T(512)S(1)}, s32[]{:T(128)}, /*index=5*/s32[]{:T(128)}) while((s32[]{:T(128)}, bf16[512,1024]{1,0:T(8,128)(2,1)S(1)}, s32[512,4]{0,1:T(4,128)S(1)}, s32[512]{0:T(512)S(1)}, s32[]{:T(128)}, /*index=5*/s32[]{:T(128)}) %tuple.57), condition=%wide.region_2.2_spmd.clone, body=%wide.region_1.1_spmd.clone.sunk | while | flops 4194819 | bytes 2106463 | solution.py:23
  31.9 1.4 %fusion.34 = bf16[8,512,128]{2,1,0:T(8,128)(2,1)S(1)} fusion(bf16[8,512,128]{2,1,0:T(8,128)(2,1)S(1)} %get-tuple-element.282, s32[]{:T(128)S(6)} %copy.26, bf16[512,1024]{1,0:T(8,128)(2,1)S(1)} %get-tuple-element.248, bf16[8,1024,128]{2,1,0:T(8,128)(2,1)} %get-tuple-element.294), kind=kOutput, calls=%fused_computation.9.clone.1 | convolution fusion | flops 134283264 | bytes 1442816 | tf_op jit(solution)/shard_map/while/body/eval_jaxpr/while/body/eval_jaxpr/dot_general | solution.py:24
  34.8 2.7 %while.33 = (s32[]{:T(128)}, bf16[512,1024]{1,0:T(8,128)(2,1)S(1)}, s32[512,4]{0,1:T(4,128)S(1)}, s32[512]{0:T(512)S(1)}, s32[]{:T(128)}, /*index=5*/s32[]{:T(128)}) while((s32[]{:T(128)}, bf16[512,1024]{1,0:T(8,128)(2,1)S(1)}, s32[512,4]{0,1:T(4,128)S(1)}, s32[512]{0:T(512)S(1)}, s32[]{:T(128)}, /*index=5*/s32[]{:T(128)}) %tuple.57), condition=%wide.region_2.2_spmd.clone, body=%wide.region_1.1_spmd.clone.sunk | while | flops 4194819 | bytes 2106463 | solution.py:23
  37.4 1.4 %fusion.34 = bf16[8,512,128]{2,1,0:T(8,128)(2,1)S(1)} fusion(bf16[8,512,128]{2,1,0:T(8,128)(2,1)S(1)} %get-tuple-element.282, s32[]{:T(128)S(6)} %copy.26, bf16[512,1024]{1,0:T(8,128)(2,1)S(1)} %get-tuple-element.248, bf16[8,1024,128]{2,1,0:T(8,128)(2,1)} %get-tuple-element.294), kind=kOutput, calls=%fused_computation.9.clone.1 | convolution fusion | flops 134283264 | bytes 1442816 | tf_op jit(solution)/shard_map/while/body/eval_jaxpr/while/body/eval_jaxpr/dot_general | solution.py:24
  40.3 2.7 %while.33 = (s32[]{:T(128)}, bf16[512,1024]{1,0:T(8,128)(2,1)S(1)}, s32[512,4]{0,1:T(4,128)S(1)}, s32[512]{0:T(512)S(1)}, s32[]{:T(128)}, /*index=5*/s32[]{:T(128)}) while((s32[]{:T(128)}, bf16[512,1024]{1,0:T(8,128)(2,1)S(1)}, s32[512,4]{0,1:T(4,128)S(1)}, s32[512]{0:T(512)S(1)}, s32[]{:T(128)}, /*index=5*/s32[]{:T(128)}) %tuple.57), condition=%wide.region_2.2_spmd.clone, body=%wide.region_1.1_spmd.clone.sunk | while | flops 4194819 | bytes 2106463 | solution.py:23
  43.0 1.4 %fusion.34 = bf16[8,512,128]{2,1,0:T(8,128)(2,1)S(1)} fusion(bf16[8,512,128]{2,1,0:T(8,128)(2,1)S(1)} %get-tuple-element.282, s32[]{:T(128)S(6)} %copy.26, bf16[512,1024]{1,0:T(8,128)(2,1)S(1)} %get-tuple-element.248, bf16[8,1024,128]{2,1,0:T(8,128)(2,1)} %get-tuple-element.294), kind=kOutput, calls=%fused_computation.9.clone.1 | convolution fusion | flops 134283264 | bytes 1442816 | tf_op jit(solution)/shard_map/while/body/eval_jaxpr/while/body/eval_jaxpr/dot_general | solution.py:24
  44.5 1.3 %copy.9 = bf16[8,32,16,128]{3,2,0,1:T(8,128)(2,1)} copy(bf16[8,32,16,128]{3,2,1,0:T(8,128)(2,1)S(1)} %bitcast.52) | data formatting | bytes 2097152 | tf_op jit(solution)/shard_map/reshape | solution.py:42
  45.8 7.3 %all-to-all-start = ((bf16[8,32,16,128]{3,2,0,1:T(8,128)(2,1)}), bf16[8,32,16,128]{3,2,0,1:T(8,128)(2,1)S(1)}, u32[]{:S(2)}, u32[]{:S(2)}) async-start(bf16[8,32,16,128]{3,2,0,1:T(8,128)(2,1)} %copy.9), calls=%async_computation | async-start | bytes 2097152 | tf_op jit(solution)/shard_map/all_to_all | solution.py:52
  53.2 26.6 %all-to-all-done = bf16[8,32,16,128]{3,2,0,1:T(8,128)(2,1)S(1)} async-done(((bf16[8,32,16,128]{3,2,0,1:T(8,128)(2,1)}), bf16[8,32,16,128]{3,2,0,1:T(8,128)(2,1)S(1)}, u32[]{:S(2)}, u32[]{:S(2)}) %all-to-all-start) | async-done | bytes 1048608 | tf_op jit(solution)/shard_map/all_to_all | solution.py:52
  81.8 1.1 %copy.16 = bf16[2,8,128,128]{3,1,2,0:T(8,128)(2,1)} copy(bf16[2,8,128,128]{3,2,1,0:T(8,128)(2,1)S(1)} %bitcast.54) | data formatting | bytes 1048576
  (135 shorter events, 31.4 us)
Async XLA Ops:
  44.5 8.6 %copy-start.2 = (bf16[16,128]{1,0:T(8,128)(2,1)S(1)}, bf16[16,128]{1,0:T(8,128)(2,1)}, u32[]{:S(2)}) copy-start(bf16[16,128]{1,0:T(8,128)(2,1)} %param.15) | copy-start | bytes 12292
  44.5 8.7 %copy-start = (bf16[128,257]{0,1:T(8,128)(2,1)S(1)}, bf16[128,257]{0,1:T(8,128)(2,1)}, u32[]{:S(2)}) copy-start(bf16[128,257]{0,1:T(8,128)(2,1)} %param.16) | copy-start | bytes 197380
  44.5 8.7 %copy-start.1 = (bf16[128,257]{0,1:T(8,128)(2,1)S(1)}, bf16[128,257]{0,1:T(8,128)(2,1)}, u32[]{:S(2)}) copy-start(bf16[128,257]{0,1:T(8,128)(2,1)} %param.17) | copy-start | bytes 197380
  45.8 34.1 %all-to-all-start = ((bf16[8,32,16,128]{3,2,0,1:T(8,128)(2,1)}), bf16[8,32,16,128]{3,2,0,1:T(8,128)(2,1)S(1)}, u32[]{:S(2)}, u32[]{:S(2)}) async-start(bf16[8,32,16,128]{3,2,0,1:T(8,128)(2,1)} %copy.9), calls=%async_computation | async-start | bytes 2097152 | tf_op jit(solution)/shard_map/all_to_all | solution.py:52
  79.9 0.8 copy-start.3
where the time goes:
time: 84.4 us; the launch traced here: 83 us
  waiting for transfers between devices  26.6 us (32%)
  other arithmetic  19.9 us (24%)
  local copies, waits for them, and re-layouts  14.9 us (18%)
  matrix products  12.7 us (15%)
  starting transfers between devices  7.33 us (9%)
  loops' own time  1.39 us (2%)
    all_to_all x1, waiting for transfers between devices, shards(): lax.all_to_all(blocks, ('hst', 'row', 'col'), split_axis=1, concat_axis=0...  26.6 us
    add x32, other arithmetic, add_ids(): return counts + hit.astype(jnp.bfloat16)  19.7 us
    dot_general x8, matrix products, one_block(): jnp.dot(counts, table, preferred_element_type=jnp.float32)  11.5 us
    all_to_all x1, starting transfers between devices, shards(): lax.all_to_all(blocks, ('hst', 'row', 'col'), split_axis=1, concat_axis=0...  7.33 us
    dynamic_slice x8, local copies, waits for them, and re-layouts, shards(): lax.map(lambda items: pool_table(items[0], items[1], items[2], bag_size),...  5.78 us
    squeeze x8, local copies, waits for them, and re-layouts, pool_table(): pooled = lax.map(one_block, (grouped_ids, grouped_lens))  5.62 us
  transfers between devices with their start and end apart: 1, of which 1 were waited for; matrix products, arithmetic and copies ran while one was open for 0% of the time, Pallas kernels for 0%

commit v1 on v0

v1 whole, which is shorter than its diff:
```python
import jax
import jax.numpy as jnp
from jax import lax
from jax.experimental import pallas as pl
from jax.experimental.pallas import tpu as pltpu
from jax.sharding import PartitionSpec as P

AXES = ("hst", "row", "col")
ROW_BLOCK = 256
SAMPLE_BLOCK = 512


def pool_kernel(ids_ref, lens_ref, table_ref, out_ref):
    table = pl.program_id(0)
    bag_size, samples = ids_ref.shape[1], ids_ref.shape[2]
    rows = table_ref.shape[1]
    one = jnp.ones((), jnp.bfloat16)
    zero = jnp.zeros((), jnp.bfloat16)
    ids = ids_ref[0]
    used = lax.broadcasted_iota(jnp.int32, ids.shape, 0) < lens_ref[pl.ds(table, 1), :]
    ids = jnp.where(used, ids, -1)
    row_iota = lax.broadcasted_iota(jnp.int32, (ROW_BLOCK, samples), 0).astype(jnp.float32).astype(jnp.bfloat16)
    total = None
    for start in range(0, rows, ROW_BLOCK):
        here = (ids - start).astype(jnp.float32).astype(jnp.bfloat16)
        counts = None
        for position in range(bag_size):
            hit = jnp.where(here[position : position + 1, :] == row_iota, one, zero)
            counts = hit if counts is None else counts + hit
        part = lax.dot_general(
            table_ref[0, start : start + ROW_BLOCK, :],
            counts,
            (((0,), (0,)), ((), ())),
            preferred_element_type=jnp.float32,
        )
        total = part if total is None else total + part
    out_ref[...] = total.T.astype(jnp.bfloat16).reshape(out_ref.shape)


def pool(tables, ids, lens, devices):
    tab_dev, rows, width = tables.shape
    bag_size, samples = ids.shape[1], ids.shape[2]
    own = samples // devices
    block = min(SAMPLE_BLOCK, samples)
    return pl.pallas_call(
        pool_kernel,
        grid=(tab_dev, samples // block),
        in_specs=[
            pl.BlockSpec((1, bag_size, block), lambda t, s: (t, 0, s)),
            pl.BlockSpec((tab_dev, block), lambda t, s: (0, s)),
            pl.BlockSpec((1, rows, width), lambda t, s: (t, 0, 0)),
        ],
        out_specs=pl.BlockSpec((block // own, 1, own, width), lambda t, s: (s, t, 0, 0)),
        out_shape=jax.ShapeDtypeStruct((devices, tab_dev, own, width), jnp.bfloat16),
        cost_estimate=pl.CostEstimate(
            flops=2 * tab_dev * rows * samples * width,
            bytes_accessed=2 * (tables.size + tab_dev * samples * width),
            transcendentals=0,
        ),
        name="pool",
    )(ids, lens, tables)


def shards(tables, indices, lengths, table_slot, dense_feature, left_proj, right_proj):
    tab_dev, all_samples, bag_size = indices.shape
    feature_width = tables.shape[2]
    devices = lax.axis_size(AXES)
    own_samples = all_samples // devices
    proj_rows = left_proj.shape[0]
    tables_total = left_proj.shape[1] - 1
    blocks = pool(tables, indices.transpose(0, 2, 1), lengths, devices)
    positions = jnp.arange(tables_total, dtype=jnp.int32)
    projections = jnp.concatenate([left_proj, right_proj], axis=0)
    selector = (table_slot[:, None] == positions[None, :]).astype(jnp.bfloat16)
    proj_here = jnp.dot(projections[:, 1:], selector, preferred_element_type=jnp.float32).astype(jnp.bfloat16)
    received = lax.all_to_all(blocks, AXES, split_axis=0, concat_axis=0, tiled=True)
    flattened = received.reshape(tables_total, own_samples * feature_width)
    mixed_all = jnp.dot(proj_here, flattened, preferred_element_type=jnp.float32)
    mixed_all = mixed_all.reshape(2 * proj_rows, own_samples, feature_width)
    dense_column = projections[:, 0].astype(jnp.float32)
    mixed_all = mixed_all + dense_column[:, None, None] * dense_feature[None].astype(jnp.float32)
    mixed_all = mixed_all.astype(jnp.bfloat16)
    left_side = mixed_all[:proj_rows]
    right_side = mixed_all[proj_rows:]
    products = jnp.einsum("kbe,lbe->bkl", left_side, right_side, preferred_element_type=jnp.float32)
    products = products * (1.0 / feature_width)
    return products.reshape(own_samples, proj_rows * proj_rows).astype(jnp.bfloat16)


def solution(mesh):
    in_specs = (
        P(AXES, None, None),
        P(AXES, None, None),
        P(AXES, None),
        P(),
        P(AXES, None),
        P(),
        P(),
    )
    out_specs = P(AXES, None)
    return jax.shard_map(shards, mesh=mesh, in_specs=in_specs, out_specs=out_specs, check_vma=False)
```

time: 84.4 us -> 45.9 us (0.54); the launches traced: 83 us -> 45.5 us
  other arithmetic: 19.9 us -> 0.01 us
  local copies, waits for them, and re-layouts: 14.9 us -> 1.98 us
  matrix products: 12.7 us -> 1.14 us
  Pallas kernels: 0 us -> 8.34 us
  loops' own time: 1.39 us -> 0 us
    add x33 -> x0, other arithmetic: 19.7 us -> none  [the longest x32 19.7 us: add_ids(): return counts + hit.astype(jnp.bfloat16)]
    dot_general x8 -> x0, matrix products: 11.5 us -> none  [one_block(): jnp.dot(counts, table, preferred_element_type=jnp.float32)]
    pallas_call x0 -> x1, Pallas kernels: none -> 8.34 us  [pool(): pl.pallas_call(pool_kernel, grid=(tab_dev, samples // block), in_specs=[p...]
    dynamic_slice x40 -> x0, local copies, waits for them, and re-layouts: 6.01 us -> none  [the longest x8 5.78 us: shards(): lax.map(lambda items: pool_table(items[0], items[1], items[2], bag_size),...]
    squeeze x8 -> x0, local copies, waits for them, and re-layouts: 5.62 us -> none  [pool_table(): pooled = lax.map(one_block, (grouped_ids, grouped_lens))]
    another operation x9 -> x0, loops' own time: 1.39 us -> none  [the longest x8 1.13 us: one_block(): counts = lax.fori_loop(0, bag_size, add_ids, counts)]
    reshape x1 -> x0, local copies, waits for them, and re-layouts: 1.26 us -> none  [shards(): blocks = pooled.reshape(tab_dev, devices, own_samples, feature_width)]
where the time goes in v1:
time: 45.9 us; the launch traced here: 45.5 us
  waiting for transfers between devices  26.6 us (58%)
  Pallas kernels  8.34 us (18%)
  starting transfers between devices  7.32 us (16%)
  local copies, waits for them, and re-layouts  1.98 us (4%)
  matrix products  1.14 us (2%)
    all_to_all x1, waiting for transfers between devices, shards(): lax.all_to_all(blocks, AXES, split_axis=0, concat_axis=0, tiled=True)  26.6 us
    pallas_call x1, Pallas kernels, pool(): pl.pallas_call(pool_kernel, grid=(tab_dev, samples // block), in_specs=[p...  8.34 us
    all_to_all x1, starting transfers between devices, shards(): lax.all_to_all(blocks, AXES, split_axis=0, concat_axis=0, tiled=True)  7.32 us
    unnamed x11, local copies, waits for them, and re-layouts  1.44 us
  transfers between devices with their start and end apart: 1, of which 1 were waited for; matrix products, arithmetic and copies ran while one was open for 0% of the time, Pallas kernels for 0%

profile of v1, /device:TPU:0, one launch (start us, length us, event | category | flops | bytes accessed | tf_op | source)
XLA Modules:
  0.0 45.5 jit_solution(6890467809470557775)
XLA Ops:
  0.0 0.0 copy-start.2
  0.0 0.0 copy-start
  0.0 8.3 %pool.1 = bf16[32,8,16,128]{3,2,1,0:T(8,128)(2,1)} custom-call(s32[8,4,512]{2,1,0:T(4,128)} %bitcast.24, s32[8,512]{1,0:T(8,128)} %lens_ref.1, bf16[8,1024,128]{2,1,0:T(8,128)(2,1)} %table_ref.1), custom_call_target="tpu_custom_call" | custom-call | flops 1073741824 | bytes 3145728 | tf_op jit(solution)/shard_map/pool/pallas_call | solution.py:45
  8.3 0.0 copy-start.1
  8.3 7.3 %all-to-all-start = ((bf16[32,8,16,128]{3,2,1,0:T(8,128)(2,1)}), bf16[32,8,16,128]{3,2,1,0:T(8,128)(2,1)S(1)}, u32[]{:S(2)}, u32[]{:S(2)}) async-start(bf16[32,8,16,128]{3,2,1,0:T(8,128)(2,1)} %pool.1), calls=%async_computation | async-start | bytes 2097152 | tf_op jit(solution)/shard_map/all_to_all | solution.py:76
  15.7 0.0 copy-done.2
  15.7 0.0 copy-done
  15.7 0.0 copy-done.1
  15.8 0.0 copy-start.3
  15.8 26.6 %all-to-all-done = bf16[32,8,16,128]{3,2,1,0:T(8,128)(2,1)S(1)} async-done(((bf16[32,8,16,128]{3,2,1,0:T(8,128)(2,1)}), bf16[32,8,16,128]{3,2,1,0:T(8,128)(2,1)S(1)}, u32[]{:S(2)}, u32[]{:S(2)}) %all-to-all-start) | async-done | bytes 1048608 | tf_op jit(solution)/shard_map/all_to_all | solution.py:76
  42.4 0.3 copy.13
  42.7 0.5 %copy.8 = bf16[2048,256]{1,0:T(8,128)(2,1)S(1)} copy(bf16[2048,256]{0,1:T(8,128)(2,1)S(1)} %bitcast.20) | data formatting | bytes 2097152 | tf_op jit(solution)/shard_map/dot_general | solution.py:78
  43.2 0.0 copy-done.3
  43.3 0.7 %add_convert_fusion = bf16[256,16,128]{2,0,1:T(8,128)(2,1)S(1)} fusion(bf16[16,128,256]{2,1,0:T(8,128)(2,1)S(1)} %bitcast.21, f32[16,128]{1,0:T(8,128)S(1)} %convert_element_type.30, f32[256]{0:T(256)S(1)} %bitcast.23, bf16[256,257]{0,1:T(8,128)(2,1)S(1)} %constant_dynamic-update-slice_fusion, s32[256]{0:T(256)S(1)} %copy-done.3), kind=kOutput, calls=%fused_computation | convolution fusion | flops 303693824 | bytes 2238464 | tf_op jit(solution)/shard_map/dot_general | solution.py:78
  43.9 0.5 %fusion = bf16[16,128,128]{2,1,0:T(8,128)(2,1)S(1)} fusion(bf16[256,16,128]{2,0,1:T(8,128)(2,1)S(1)} %add_convert_fusion), kind=kOutput, calls=%fused_computation.2 | convolution fusion | flops 67633152 | bytes 1572864 | tf_op jit(solution)/shard_map/kbe,lbe->bkl/dot_general | solution.py:85
  44.4 1.1 %copy.14 = bf16[2,8,128,128]{3,1,2,0:T(8,128)(2,1)} copy(bf16[2,8,128,128]{3,2,1,0:T(8,128)(2,1)S(1)} %bitcast.22) | data formatting | bytes 1048576
  (4 shorter events, 0.0 us)
Async XLA Ops:
  0.0 15.7 %copy-start.2 = (bf16[16,128]{1,0:T(8,128)(2,1)S(1)}, bf16[16,128]{1,0:T(8,128)(2,1)}, u32[]{:S(2)}) copy-start(bf16[16,128]{1,0:T(8,128)(2,1)} %param.11) | copy-start | bytes 12292
  0.0 15.7 %copy-start = (bf16[128,257]{0,1:T(8,128)(2,1)S(1)}, bf16[128,257]{0,1:T(8,128)(2,1)}, u32[]{:S(2)}) copy-start(bf16[128,257]{0,1:T(8,128)(2,1)} %param.12) | copy-start | bytes 197380
  8.3 7.4 %copy-start.1 = (bf16[128,257]{0,1:T(8,128)(2,1)S(1)}, bf16[128,257]{0,1:T(8,128)(2,1)}, u32[]{:S(2)}) copy-start(bf16[128,257]{0,1:T(8,128)(2,1)} %param.13) | copy-start | bytes 197380
  8.3 34.1 %all-to-all-start = ((bf16[32,8,16,128]{3,2,1,0:T(8,128)(2,1)}), bf16[32,8,16,128]{3,2,1,0:T(8,128)(2,1)S(1)}, u32[]{:S(2)}, u32[]{:S(2)}) async-start(bf16[32,8,16,128]{3,2,1,0:T(8,128)(2,1)} %pool.1), calls=%async_computation | async-start | bytes 2097152 | tf_op jit(solution)/shard_map/all_to_all | solution.py:76
  15.8 27.5 %copy-start.3 = (s32[256]{0:T(256)S(1)}, s32[256]{0:T(256)}, u32[]{:S(2)}) copy-start(s32[256]{0:T(256)} %param.10) | copy-start | bytes 3076

commit v2 on v1

--- a/solution.py
+++ b/solution.py
@@ -7,50 +7,63 @@
 
 AXES = ("hst", "row", "col")
 ROW_BLOCK = 256
-SAMPLE_BLOCK = 512
+SAMPLE_BLOCK = 256
+TABLE_BLOCK = 4
 
 
 def pool_kernel(ids_ref, lens_ref, table_ref, out_ref):
-    table = pl.program_id(0)
-    bag_size, samples = ids_ref.shape[1], ids_ref.shape[2]
+    tables, bag_size, samples = ids_ref.shape
     rows = table_ref.shape[1]
-    one = jnp.ones((), jnp.bfloat16)
+    own = out_ref.shape[2]
+    first = pl.program_id(0) * tables
+    block = min(SAMPLE_BLOCK, samples)
     zero = jnp.zeros((), jnp.bfloat16)
-    ids = ids_ref[0]
-    used = lax.broadcasted_iota(jnp.int32, ids.shape, 0) < lens_ref[pl.ds(table, 1), :]
-    ids = jnp.where(used, ids, -1)
-    row_iota = lax.broadcasted_iota(jnp.int32, (ROW_BLOCK, samples), 0).astype(jnp.float32).astype(jnp.bfloat16)
-    total = None
-    for start in range(0, rows, ROW_BLOCK):
-        here = (ids - start).astype(jnp.float32).astype(jnp.bfloat16)
-        counts = None
-        for position in range(bag_size):
-            hit = jnp.where(here[position : position + 1, :] == row_iota, one, zero)
-            counts = hit if counts is None else counts + hit
-        part = lax.dot_general(
-            table_ref[0, start : start + ROW_BLOCK, :],
-            counts,
-            (((0,), (0,)), ((), ())),
-            preferred_element_type=jnp.float32,
-        )
-        total = part if total is None else total + part
-    out_ref[...] = total.T.astype(jnp.bfloat16).reshape(out_ref.shape)
+    row_iota = lax.broadcasted_iota(jnp.int32, (ROW_BLOCK, block), 0).astype(jnp.float32).astype(jnp.bfloat16)
+    for table in range(tables):
+        for at in range(0, samples, block):
+            bag = ids_ref[table, :, at : at + block]
+            used = lax.broadcasted_iota(jnp.int32, bag.shape, 0) < lens_ref[pl.ds(first + table, 1), at : at + block]
+            bag = jnp.where(used, bag, -1)
+            ids = [bag[j : j + 1] for j in range(bag_size)]
+            times = [jnp.ones_like(ids[0]) for _ in range(bag_size)]
+            for later in range(1, bag_size):
+                for earlier in range(later):
+                    same = ids[earlier] == ids[later]
+                    times[earlier] = times[earlier] + jnp.where(same, times[later], 0)
+                    ids[later] = jnp.where(same, -1, ids[later])
+                    times[later] = jnp.where(same, 0, times[later])
+            times = [t.astype(jnp.float32).astype(jnp.bfloat16) for t in times]
+            total = None
+            for start in range(0, rows, ROW_BLOCK):
+                counts = zero
+                for j in range(bag_size):
+                    here = (ids[j] - start).astype(jnp.float32).astype(jnp.bfloat16)
+                    counts = jnp.where(here == row_iota, times[j], counts)
+                part = lax.dot_general(
+                    table_ref[table, start : start + ROW_BLOCK, :],
+                    counts,
+                    (((0,), (0,)), ((), ())),
+                    preferred_element_type=jnp.float32,
+                )
+                total = part if total is None else total + part
+            out_ref[at // own : (at + block) // own, table] = (
+                total.T.astype(jnp.bfloat16).reshape(block // own, own, total.shape[0])
+            )
 
 
 def pool(tables, ids, lens, devices):
     tab_dev, rows, width = tables.shape
     bag_size, samples = ids.shape[1], ids.shape[2]
     own = samples // devices
-    block = min(SAMPLE_BLOCK, samples)
     return pl.pallas_call(
         pool_kernel,
-        grid=(tab_dev, samples // block),
+        grid=(tab_dev // TABLE_BLOCK,),
         in_specs=[
-            pl.BlockSpec((1, bag_size, block), lambda t, s: (t, 0, s)),
-            pl.BlockSpec((tab_dev, block), lambda t, s: (0, s)),
-            pl.BlockSpec((1, rows, width), lambda t, s: (t, 0, 0)),
+            pl.BlockSpec((TABLE_BLOCK, bag_size, samples), lambda t: (t, 0, 0)),
+            pl.BlockSpec((tab_dev, samples), lambda t: (0, 0)),
+            pl.BlockSpec((TABLE_BLOCK, rows, width), lambda t: (t, 0, 0)),
         ],
-        out_specs=pl.BlockSpec((block // own, 1, own, width), lambda t, s: (s, t, 0, 0)),
+        out_specs=pl.BlockSpec((devices, TABLE_BLOCK, own, width), lambda t: (0, t, 0, 0)),
         out_shape=jax.ShapeDtypeStruct((devices, tab_dev, own, width), jnp.bfloat16),
         cost_estimate=pl.CostEstimate(
             flops=2 * tab_dev * rows * samples * width,

time: 45.9 us -> 43 us (0.937)
  Pallas kernels: 8.34 us -> 5.52 us
    pallas_call x1, Pallas kernels: 8.34 us -> 5.52 us  [pool(): pl.pallas_call(pool_kernel, grid=(tab_dev // TABLE_BLOCK,), in_specs=[pl....]
where the time goes in v2:
time: 43 us; the launch traced here: 42.7 us
  waiting for transfers between devices  26.6 us (62%)
  starting transfers between devices  7.32 us (17%)
  Pallas kernels  5.52 us (13%)
  local copies, waits for them, and re-layouts  1.98 us (5%)
  matrix products  1.14 us (3%)
    all_to_all x1, waiting for transfers between devices, shards(): lax.all_to_all(blocks, AXES, split_axis=0, concat_axis=0, tiled=True)  26.6 us
    all_to_all x1, starting transfers between devices, shards(): lax.all_to_all(blocks, AXES, split_axis=0, concat_axis=0, tiled=True)  7.32 us
    pallas_call x1, Pallas kernels, pool(): pl.pallas_call(pool_kernel, grid=(tab_dev // TABLE_BLOCK,), in_specs=[pl....  5.52 us
    unnamed x11, local copies, waits for them, and re-layouts  1.44 us
  transfers between devices with their start and end apart: 1, of which 1 were waited for; matrix products, arithmetic and copies ran while one was open for 0% of the time, Pallas kernels for 0%

profile of v2, /device:TPU:0, one launch (start us, length us, event | category | flops | bytes accessed | tf_op | source)
XLA Modules:
  0.0 42.7 jit_solution(6768079162549334519)
XLA Ops:
  0.0 0.0 copy-start.2
  0.0 0.0 copy-start
  0.0 5.5 %pool.1 = bf16[32,8,16,128]{3,2,1,0:T(8,128)(2,1)} custom-call(s32[8,4,512]{2,1,0:T(4,128)} %bitcast.24, s32[8,512]{1,0:T(8,128)} %lens_ref.1, bf16[8,1024,128]{2,1,0:T(8,128)(2,1)} %table_ref.1), custom_call_target="tpu_custom_call" | custom-call | flops 1073741824 | bytes 3145728 | tf_op jit(solution)/shard_map/pool/pallas_call | solution.py:58
  5.5 0.0 copy-start.1
  5.5 7.3 %all-to-all-start = ((bf16[32,8,16,128]{3,2,1,0:T(8,128)(2,1)}), bf16[32,8,16,128]{3,2,1,0:T(8,128)(2,1)S(1)}, u32[]{:S(2)}, u32[]{:S(2)}) async-start(bf16[32,8,16,128]{3,2,1,0:T(8,128)(2,1)} %pool.1), calls=%async_computation | async-start | bytes 2097152 | tf_op jit(solution)/shard_map/all_to_all | solution.py:89
  12.9 0.0 copy-done.2
  12.9 0.0 copy-done
  12.9 0.0 copy-done.1
  13.0 0.0 copy-start.3
  13.0 26.6 %all-to-all-done = bf16[32,8,16,128]{3,2,1,0:T(8,128)(2,1)S(1)} async-done(((bf16[32,8,16,128]{3,2,1,0:T(8,128)(2,1)}), bf16[32,8,16,128]{3,2,1,0:T(8,128)(2,1)S(1)}, u32[]{:S(2)}, u32[]{:S(2)}) %all-to-all-start) | async-done | bytes 1048608 | tf_op jit(solution)/shard_map/all_to_all | solution.py:89
  39.6 0.3 copy.13
  39.9 0.5 %copy.8 = bf16[2048,256]{1,0:T(8,128)(2,1)S(1)} copy(bf16[2048,256]{0,1:T(8,128)(2,1)S(1)} %bitcast.20) | data formatting | bytes 2097152 | tf_op jit(solution)/shard_map/dot_general | solution.py:91
  40.4 0.0 copy-done.3
  40.4 0.7 %add_convert_fusion = bf16[256,16,128]{2,0,1:T(8,128)(2,1)S(1)} fusion(bf16[16,128,256]{2,1,0:T(8,128)(2,1)S(1)} %bitcast.21, f32[16,128]{1,0:T(8,128)S(1)} %convert_element_type.30, f32[256]{0:T(256)S(1)} %bitcast.23, bf16[256,257]{0,1:T(8,128)(2,1)S(1)} %constant_dynamic-update-slice_fusion, s32[256]{0:T(256)S(1)} %copy-done.3), kind=kOutput, calls=%fused_computation | convolution fusion | flops 303693824 | bytes 2238464 | tf_op jit(solution)/shard_map/dot_general | solution.py:91
  41.1 0.5 %fusion = bf16[16,128,128]{2,1,0:T(8,128)(2,1)S(1)} fusion(bf16[256,16,128]{2,0,1:T(8,128)(2,1)S(1)} %add_convert_fusion), kind=kOutput, calls=%fused_computation.2 | convolution fusion | flops 67633152 | bytes 1572864 | tf_op jit(solution)/shard_map/kbe,lbe->bkl/dot_general | solution.py:98
  41.6 1.1 %copy.14 = bf16[2,8,128,128]{3,1,2,0:T(8,128)(2,1)} copy(bf16[2,8,128,128]{3,2,1,0:T(8,128)(2,1)S(1)} %bitcast.22) | data formatting | bytes 1048576
  (4 shorter events, 0.0 us)
Async XLA Ops:
  0.0 12.9 %copy-start.2 = (bf16[16,128]{1,0:T(8,128)(2,1)S(1)}, bf16[16,128]{1,0:T(8,128)(2,1)}, u32[]{:S(2)}) copy-start(bf16[16,128]{1,0:T(8,128)(2,1)} %param.11) | copy-start | bytes 12292
  0.0 12.9 %copy-start = (bf16[128,257]{0,1:T(8,128)(2,1)S(1)}, bf16[128,257]{0,1:T(8,128)(2,1)}, u32[]{:S(2)}) copy-start(bf16[128,257]{0,1:T(8,128)(2,1)} %param.12) | copy-start | bytes 197380
  5.5 7.4 %copy-start.1 = (bf16[128,257]{0,1:T(8,128)(2,1)S(1)}, bf16[128,257]{0,1:T(8,128)(2,1)}, u32[]{:S(2)}) copy-start(bf16[128,257]{0,1:T(8,128)(2,1)} %param.13) | copy-start | bytes 197380
  5.5 34.1 %all-to-all-start = ((bf16[32,8,16,128]{3,2,1,0:T(8,128)(2,1)}), bf16[32,8,16,128]{3,2,1,0:T(8,128)(2,1)S(1)}, u32[]{:S(2)}, u32[]{:S(2)}) async-start(bf16[32,8,16,128]{3,2,1,0:T(8,128)(2,1)} %pool.1), calls=%async_computation | async-start | bytes 2097152 | tf_op jit(solution)/shard_map/all_to_all | solution.py:89
  13.0 27.5 %copy-start.3 = (s32[256]{0:T(256)S(1)}, s32[256]{0:T(256)}, u32[]{:S(2)}) copy-start(s32[256]{0:T(256)} %param.10) | copy-start | bytes 3076

commit v3 on v2

v3 whole, which is shorter than its diff:
```python
import functools

import jax
import jax.numpy as jnp
from jax import lax
from jax.experimental import pallas as pl
from jax.experimental.pallas import tpu as pltpu
from jax.sharding import PartitionSpec as P

AXES = ("hst", "row", "col")
PLANE = ("hst", "row")
LINE = "col"
ROW_BLOCK = 256
SAMPLE_BLOCK = 256
VMEM_LIMIT = 24 * 1024 * 1024
EARLY = 3
TABLE_BLOCK = 4


def pool_table(ids_ref, lens_ref, table_ref, table, slot, write):
    bag_size, samples = ids_ref.shape[1:]
    rows = table_ref.shape[1]
    block = min(SAMPLE_BLOCK, samples)
    zero = jnp.zeros((), jnp.bfloat16)
    row_iota = lax.broadcasted_iota(jnp.int32, (ROW_BLOCK, block), 0).astype(jnp.float32).astype(jnp.bfloat16)
    for at in range(0, samples, block):
        bag = ids_ref[slot, :, at : at + block]
        used = lax.broadcasted_iota(jnp.int32, bag.shape, 0) < lens_ref[pl.ds(table, 1), at : at + block]
        bag = jnp.where(used, bag, -1)
        ids = [bag[j : j + 1] for j in range(bag_size)]
        times = [jnp.ones_like(ids[0]) for _ in range(bag_size)]
        for later in range(1, bag_size):
            for earlier in range(later):
                same = ids[earlier] == ids[later]
                times[earlier] = times[earlier] + jnp.where(same, times[later], 0)
                ids[later] = jnp.where(same, -1, ids[later])
                times[later] = jnp.where(same, 0, times[later])
        times = [t.astype(jnp.float32).astype(jnp.bfloat16) for t in times]
        total = None
        for start in range(0, rows, ROW_BLOCK):
            counts = zero
            for j in range(bag_size):
                here = (ids[j] - start).astype(jnp.float32).astype(jnp.bfloat16)
                counts = jnp.where(here == row_iota, times[j], counts)
            part = lax.dot_general(
                table_ref[slot, start : start + ROW_BLOCK, :],
                counts,
                (((0,), (0,)), ((), ())),
                preferred_element_type=jnp.float32,
            )
            total = part if total is None else total + part
        write(at, block, total.T.astype(jnp.bfloat16))


def pool_kernel(early, steps, ids_ref, lens_ref, table_ref, *refs):
    columns = (len(refs) - 4) // 2
    near, far = refs[:columns], refs[columns]
    near_bufs, (far_buf, held, sems) = refs[columns + 1 : 2 * columns + 1], refs[2 * columns + 1 :]
    step_tables = table_ref.shape[0]
    own, width = held.shape[1:]
    plane, column = lax.axis_index(PLANE), lax.axis_index(LINE)
    copies = [pltpu.make_async_copy(near_bufs[r], near[r], sems.at[r]) for r in range(columns)]
    for step in range(steps):

        @pl.when(pl.program_id(0) == step)
        def _(step=step):
            for slot in range(step_tables):
                table = step * step_tables + slot

                def write(at, block, pooled):
                    pooled = pooled.reshape(block // own, own, width)
                    if table < early:
                        held[at // own : (at + block) // own] = pooled
                    else:
                        far_buf[at // own : (at + block) // own, table - early] = pooled

                pool_table(ids_ref, lens_ref, table_ref, table, slot, write)
                if table < early:
                    for r in range(columns):
                        for p in range(near_bufs[r].shape[0]):
                            device = lax.bitwise_xor(plane, p) * columns + lax.bitwise_xor(column, r)
                            near_bufs[r][p, table] = held[device]
                if table == early - 1:
                    for copy in copies:
                        copy.start()
            if step == steps - 1:
                last = pltpu.make_async_copy(far_buf, far, sems.at[columns])
                last.start()
                for copy in copies:
                    copy.wait()
                last.wait()


def pool(tables, ids, lens, early, planes, columns):
    tab_dev, rows, width = tables.shape
    bag_size, samples = ids.shape[1], ids.shape[2]
    devices = planes * columns
    own = samples // devices
    steps = tab_dev // TABLE_BLOCK
    near = (planes, early, own, width)
    far = (devices, tab_dev - early, own, width)
    shapes = [near] * columns + [far]
    outs = pl.pallas_call(
        functools.partial(pool_kernel, early, steps),
        grid=(steps,),
        in_specs=[
            pl.BlockSpec((TABLE_BLOCK, bag_size, samples), lambda t: (t, 0, 0)),
            pl.BlockSpec((tab_dev, samples), lambda t: (0, 0)),
            pl.BlockSpec((TABLE_BLOCK, rows, width), lambda t: (t, 0, 0)),
        ],
        out_specs=[pl.BlockSpec(memory_space=pl.ANY)] * len(shapes),
        out_shape=[jax.ShapeDtypeStruct(shape, jnp.bfloat16) for shape in shapes],
        scratch_shapes=[pltpu.VMEM(shape, jnp.bfloat16) for shape in shapes]
        + [pltpu.VMEM((devices, own, width), jnp.bfloat16), pltpu.SemaphoreType.DMA((len(shapes),))],
        cost_estimate=pl.CostEstimate(
            flops=2 * tab_dev * rows * samples * width,
            bytes_accessed=2 * tab_dev * (rows + samples) * width,
            transcendentals=0,
        ),
        name="pool",
    )(ids, lens, tables)
    return outs[:-1], outs[-1]


def by_sample(blocks):
    own, width = blocks.shape[-2:]
    return jnp.swapaxes(blocks.reshape(-1, own, width), 0, 1)


def gather_kernel(*refs):
    out_ref = refs[-1]
    at = 0
    for ref in refs[:-1]:
        part = by_sample(ref[...])
        out_ref[:, at : at + part.shape[1]] = part
        at += part.shape[1]


def gather_early(pieces):
    own, width = pieces[0].shape[-2:]
    rows = sum(piece.size for piece in pieces) // (own * width)
    vmem = pl.BlockSpec(memory_space=pltpu.VMEM)
    return pl.pallas_call(
        gather_kernel,
        in_specs=[vmem] * len(pieces),
        out_specs=vmem,
        out_shape=jax.ShapeDtypeStruct((own, rows, width), jnp.bfloat16),
        compiler_params=pltpu.CompilerParams(vmem_limit_bytes=VMEM_LIMIT),
        name="gather_early",
    )(*pieces)


def interact_kernel(early_ref, late_ref, proj_ref, dense_proj_ref, dense_ref, out_ref):
    own, width = dense_ref.shape
    proj_rows = proj_ref.shape[0] // 2
    late = by_sample(late_ref[...])
    features = jnp.concatenate([jnp.concatenate([early_ref[b], late[b]], 0) for b in range(own)], 1)
    mixed = jnp.dot(proj_ref[...], features, preferred_element_type=jnp.float32)
    dense_proj = jnp.broadcast_to(dense_proj_ref[...].astype(jnp.float32), (8, 2 * proj_rows)).T[:, :1]
    dense = dense_ref[...].astype(jnp.float32)
    products = []
    for b in range(own):
        sides = (mixed[:, b * width : (b + 1) * width] + dense_proj * dense[b : b + 1]).astype(jnp.bfloat16)
        product = lax.dot_general(
            sides[:proj_rows], sides[proj_rows:], (((1,), (1,)), ((), ())), preferred_element_type=jnp.float32
        )
        products.append((product * (1.0 / width)).astype(jnp.bfloat16))
    by_row = jnp.swapaxes(jnp.stack(products), 0, 1)
    for row in range(proj_rows):
        out_ref[:, row * proj_rows : (row + 1) * proj_rows] = by_row[row]


def interact(early, late, proj, dense_proj, dense):
    own, _ = dense.shape
    proj_rows = proj.shape[0] // 2
    vmem = pl.BlockSpec(memory_space=pltpu.VMEM)
    return pl.pallas_call(
        interact_kernel,
        in_specs=[vmem] * 5,
        out_specs=vmem,
        out_shape=jax.ShapeDtypeStruct((own, proj_rows * proj_rows), jnp.bfloat16),
        compiler_params=pltpu.CompilerParams(vmem_limit_bytes=VMEM_LIMIT),
        name="interact",
    )(early, late, proj, dense_proj, dense)


def shards(tables, indices, lengths, table_slot, dense_feature, left_proj, right_proj):
    tab_dev, _, _ = indices.shape
    devices = lax.axis_size(AXES)
    columns = lax.axis_size(LINE)
    planes = lax.axis_size(PLANE)
    early = EARLY
    plane, column = lax.axis_index(PLANE), lax.axis_index(LINE)

    def swap(x, axis, size, distance):
        return lax.ppermute(x, axis, [(i, i ^ distance) for i in range(size)])

    near, blocks = pool(tables, indices.transpose(0, 2, 1), lengths, early, planes, columns)
    arrived = {r: swap(near[r], LINE, columns, r) for r in range(1, columns)}
    late = lax.all_to_all(blocks, AXES, split_axis=0, concat_axis=0, tiled=True)
    stacked = [jnp.stack([near[0][p]] + [arrived[r][p] for r in range(1, columns)]) for p in range(planes)]
    pieces = [stacked[0]] + [swap(stacked[p], PLANE, planes, p) for p in range(1, planes)]
    features = gather_early(pieces)
    p, r, t = jnp.meshgrid(jnp.arange(planes), jnp.arange(columns), jnp.arange(early), indexing="ij")
    early_slots = ((plane ^ p) * columns + (column ^ r)) * tab_dev + t
    d, t = jnp.meshgrid(jnp.arange(devices), jnp.arange(early, tab_dev), indexing="ij")
    slots = jnp.concatenate([early_slots.reshape(-1), (d * tab_dev + t).reshape(-1)])
    selector = (table_slot[:, None] == slots[None, :]).astype(jnp.bfloat16)
    projections = jnp.concatenate([left_proj, right_proj], axis=0)
    proj = jnp.dot(projections[:, 1:], selector, preferred_element_type=jnp.float32).astype(jnp.bfloat16)
    dense_proj = projections[:, 0][None]
    return interact(features, late, proj, dense_proj, dense_feature)


def solution(mesh):
    in_specs = (
        P(AXES, None, None),
        P(AXES, None, None),
        P(AXES, None),
        P(),
        P(AXES, None),
        P(),
        P(),
    )
    out_specs = P(AXES, None)
    return jax.shard_map(shards, mesh=mesh, in_specs=in_specs, out_specs=out_specs, check_vma=False)
```

time: 43 us -> 38.4 us (0.89)
  waiting for transfers between devices: 26.6 us -> 9.99 us
  starting transfers between devices: 7.32 us -> 18.6 us
  Pallas kernels: 5.52 us -> 7.64 us
  matrix products: 1.14 us -> 0.28 us
  local copies, waits for them, and re-layouts: 1.98 us -> 1.14 us
    all_to_all x1, waiting for transfers between devices: 26.6 us -> 3.97 us  [shards(): late = lax.all_to_all(blocks, AXES, split_axis=0, concat_axis=0, tiled=True)]
    ppermute x0 -> x10, starting transfers between devices: none -> 12.6 us  [swap(): return lax.ppermute(x, axis, [(i, i ^ distance) for i in range(size)])]
    ppermute x0 -> x10, waiting for transfers between devices: none -> 6.02 us  [swap(): return lax.ppermute(x, axis, [(i, i ^ distance) for i in range(size)])]
    pallas_call x1 -> x3, Pallas kernels: 5.52 us -> 7.64 us  [the longest x1 5.66 us: pool(): pl.pallas_call(functools.partial(pool_kernel, early, steps), grid=(steps,...]
    unnamed x11 -> x9, local copies, waits for them, and re-layouts: 1.44 us -> 0.03 us
    all_to_all x1, starting transfers between devices: 7.32 us -> 6 us  [shards(): late = lax.all_to_all(blocks, AXES, split_axis=0, concat_axis=0, tiled=True)]
    slice x0 -> x4, local copies, waits for them, and re-layouts: none -> 0.87 us  [the longest x1 0.84 us: shards(): near[0][p]]
    dot_general x2 -> x1, matrix products: 1.14 us -> 0.28 us  [shards(): jnp.dot(projections[:, 1:], selector, preferred_element_type=jnp.float32)]
  transfers between devices with their start and end apart: 1 -> 11, of which waited for: 1 -> 6; matrix products, arithmetic and copies ran while one was open for 0% -> 5% of each run, Pallas kernels for 0% -> 0%
where the time goes in v3:
time: 38.4 us; the launch traced here: 38.2 us
  starting transfers between devices  18.6 us (48%)
  waiting for transfers between devices  9.99 us (26%)
  Pallas kernels  7.64 us (20%)
  local copies, waits for them, and re-layouts  1.14 us (3%)
    ppermute x10, starting transfers between devices, swap(): return lax.ppermute(x, axis, [(i, i ^ distance) for i in range(size)])  12.6 us
    ppermute x10, waiting for transfers between devices, swap(): return lax.ppermute(x, axis, [(i, i ^ distance) for i in range(size)])  6.02 us
    all_to_all x1, starting transfers between devices, shards(): late = lax.all_to_all(blocks, AXES, split_axis=0, concat_axis=0, tiled=True)  6 us
    pallas_call x1, Pallas kernels, pool(): pl.pallas_call(functools.partial(pool_kernel, early, steps), grid=(steps,...  5.66 us
    all_to_all x1, waiting for transfers between devices, shards(): late = lax.all_to_all(blocks, AXES, split_axis=0, concat_axis=0, tiled=True)  3.97 us
    pallas_call x1, Pallas kernels, interact(): pl.pallas_call(interact_kernel, in_specs=[vmem] * 5, out_specs=vmem, out_...  1.8 us
    slice x1, local copies, waits for them, and re-layouts, shards(): near[0][p]  0.84 us
  transfers between devices with their start and end apart: 11, of which 6 were waited for; matrix products, arithmetic and copies ran while one was open for 5% of the time, Pallas kernels for 0%

profile of v3, /device:TPU:0, one launch (start us, length us, event | category | flops | bytes accessed | tf_op | source)
XLA Modules:
  0.0 38.2 jit_solution(14135364473242435158)
XLA Ops:
  0.0 5.7 %pool.1 = (bf16[8,3,16,128]{3,2,1,0:T(8,128)(2,1)}, bf16[8,3,16,128]{3,2,1,0:T(8,128)(2,1)}, bf16[8,3,16,128]{3,2,1,0:T(8,128)(2,1)}, bf16[8,3,16,128]{3,2,1,0:T(8,128)(2,1)}, bf16[32,5,16,128]{3,2,1,0:T(8,128)(2,1)}) custom-call(s32[8,4,512]{2,1,0:T(4,128)} %bitcast.3, s32[8,512]{1,0:T(8,128)} %lens_ref.1, bf16[8,1024,128]{2,1,0:T(8,128)(2,1)} %table_ref.1), custom_call_target="tpu_custom_call" | custom-call | flops 1073741824 | bytes 3145728 | tf_op jit(solution)/shard_map/pool/pallas_call | solution.py:103
  5.7 5.2 %collective-permute-start.2 = (bf16[8,3,16,128]{3,2,1,0:T(8,128)(2,1)}, bf16[8,3,16,128]{3,2,1,0:T(8,128)(2,1)S(1)}, u32[]{:S(2)}, u32[]{:S(2)}) collective-permute-start(bf16[8,3,16,128]{3,2,1,0:T(8,128)(2,1)} %get-tuple-element.13), channel_id=1, source_target_pairs={{0,3},{1,2},{2,1},{3,0},{4,7},{5,6},{6,5},{7,4},{8,11},{9,10},{10,... | collective-permute-start | bytes 294920 | tf_op jit(solution)/shard_map/ppermute | solution.py:196
  10.8 0.6 %collective-permute-start = (bf16[8,3,16,128]{3,2,1,0:T(8,128)(2,1)}, bf16[8,3,16,128]{3,2,1,0:T(8,128)(2,1)S(1)}, u32[]{:S(2)}, u32[]{:S(2)}) collective-permute-start(bf16[8,3,16,128]{3,2,1,0:T(8,128)(2,1)} %get-tuple-element.11), channel_id=1, source_target_pairs={{0,1},{1,0},{2,3},{3,2},{4,5},{5,4},{6,7},{7,6},{8,9},{9,8},{10,11... | collective-permute-start | bytes 294920 | tf_op jit(solution)/shard_map/ppermute | solution.py:196
  11.5 6.0 %all-to-all-start = ((bf16[32,5,16,128]{3,2,1,0:T(8,128)(2,1)}), bf16[32,5,16,128]{3,2,1,0:T(8,128)(2,1)S(1)}, u32[]{:S(2)}, u32[]{:S(2)}) async-start(bf16[32,5,16,128]{3,2,1,0:T(8,128)(2,1)} %get-tuple-element.14), calls=%async_computation | async-start | bytes 1310720 | tf_op jit(solution)/shard_map/all_to_all | solution.py:200
  17.5 0.8 %fusion.4 = (bf16[1,3,16,128]{3,2,1,0:T(8,128)(2,1)S(1)}, bf16[1,3,16,128]{3,2,1,0:T(8,128)(2,1)S(1)}, bf16[1,3,16,128]{3,2,1,0:T(8,128)(2,1)S(1)}, bf16[1,3,16,...) fusion(bf16[8,3,16,128]{3,2,1,0:T(8,128)(2,1)} %get-tuple-eleme, ...), kind=kLoop, calls=%fused_computation.23 | loop fusion | bytes 196608 | tf_op jit(solution)/shard_map/slice | solution.py:201
  18.4 0.1 broadcast_add_fusion
  18.5 0.1 add.31
  18.6 0.1 iota_add_fusion
  18.7 0.1 add.28
  18.8 0.1 pad_add_fusion
  18.9 0.3 convolution_convert_fusion.proj_ref
  19.2 0.1 collective-permute-done.1
  19.4 1.8 %collective-permute-start.3 = (bf16[4,3,16,128]{3,2,1,0:T(8,128)(2,1)S(1)}, bf16[4,3,16,128]{3,2,1,0:T(8,128)(2,1)S(1)}, u32[]{:S(2)}, u32[]{:S(2)}) collective-permute-start(bf16[4,3,16,128]{3,2,1,0:T(8,128)(2,1)S(1)} %pad_maximum_fusion.1), channel_id=1, source_target_pairs={{0,4},{4,0},{8,12},{12,8},{16,20},{20,16},{24,28},{28,24},{1,5},{5... | collective-permute-start | bytes 147464 | tf_op jit(solution)/shard_map/ppermute | solution.py:196
  21.2 1.5 %collective-permute-start.4 = (bf16[4,3,16,128]{3,2,1,0:T(8,128)(2,1)S(1)}, bf16[4,3,16,128]{3,2,1,0:T(8,128)(2,1)S(1)}, u32[]{:S(2)}, u32[]{:S(2)}) collective-permute-start(bf16[4,3,16,128]{3,2,1,0:T(8,128)(2,1)S(1)} %pad_maximum_fusion.2), channel_id=1, source_target_pairs={{0,8},{4,12},{8,0},{12,4},{16,24},{20,28},{24,16},{28,20},{1,9},{5... | collective-permute-start | bytes 147464 | tf_op jit(solution)/shard_map/ppermute | solution.py:196
  22.7 0.4 %collective-permute-start.5 = (bf16[4,3,16,128]{3,2,1,0:T(8,128)(2,1)S(1)}, bf16[4,3,16,128]{3,2,1,0:T(8,128)(2,1)S(1)}, u32[]{:S(2)}, u32[]{:S(2)}) collective-permute-start(bf16[4,3,16,128]{3,2,1,0:T(8,128)(2,1)S(1)} %pad_maximum_fusion.3), channel_id=1, source_target_pairs={{0,12},{4,8},{8,4},{12,0},{16,28},{20,24},{24,20},{28,16},{1,13},{... | collective-permute-start | bytes 147464 | tf_op jit(solution)/shard_map/ppermute | solution.py:196
  23.2 1.9 %collective-permute-start.7 = (bf16[4,3,16,128]{3,2,1,0:T(8,128)(2,1)S(1)}, bf16[4,3,16,128]{3,2,1,0:T(8,128)(2,1)S(1)}, u32[]{:S(2)}, u32[]{:S(2)}) collective-permute-start(bf16[4,3,16,128]{3,2,1,0:T(8,128)(2,1)S(1)} %pad_maximum_fusion.5), channel_id=1, source_target_pairs={{0,20},{4,16},{8,28},{12,24},{16,4},{20,0},{24,12},{28,8},{1,21},{... | collective-permute-start | bytes 147464 | tf_op jit(solution)/shard_map/ppermute | solution.py:196
  25.1 1.2 %collective-permute-start.8 = (bf16[4,3,16,128]{3,2,1,0:T(8,128)(2,1)S(1)}, bf16[4,3,16,128]{3,2,1,0:T(8,128)(2,1)S(1)}, u32[]{:S(2)}, u32[]{:S(2)}) collective-permute-start(bf16[4,3,16,128]{3,2,1,0:T(8,128)(2,1)S(1)} %pad_maximum_fusion.6), channel_id=1, source_target_pairs={{0,24},{4,28},{8,16},{12,20},{16,8},{20,12},{24,0},{28,4},{1,25},{... | collective-permute-start | bytes 147464 | tf_op jit(solution)/shard_map/ppermute | solution.py:196
  26.3 0.9 %collective-permute-done.4.refs_2_ = bf16[4,3,16,128]{3,2,1,0:T(8,128)(2,1)S(1)} collective-permute-done((bf16[4,3,16,128]{3,2,1,0:T(8,128)(2,1)S(1)}, bf16[4,3,16,128]{3,2,1,0:T(8,128)(2,1)S(1)}, u32[]{:S(2)}, u32[]{:S(2)}) %collective-permute-start.4) | collective-permute-done | bytes 49184 | tf_op jit(solution)/shard_map/ppermute | solution.py:196
  27.2 2.0 %collective-permute-done.5.refs_3_ = bf16[4,3,16,128]{3,2,1,0:T(8,128)(2,1)S(1)} collective-permute-done((bf16[4,3,16,128]{3,2,1,0:T(8,128)(2,1)S(1)}, bf16[4,3,16,128]{3,2,1,0:T(8,128)(2,1)S(1)}, u32[]{:S(2)}, u32[]{:S(2)}) %collective-permute-start.5) | collective-permute-done | bytes 49184 | tf_op jit(solution)/shard_map/ppermute | solution.py:196
  29.2 0.8 %collective-permute-done.8.refs_6_ = bf16[4,3,16,128]{3,2,1,0:T(8,128)(2,1)S(1)} collective-permute-done((bf16[4,3,16,128]{3,2,1,0:T(8,128)(2,1)S(1)}, bf16[4,3,16,128]{3,2,1,0:T(8,128)(2,1)S(1)}, u32[]{:S(2)}, u32[]{:S(2)}) %collective-permute-start.8) | collective-permute-done | bytes 49184 | tf_op jit(solution)/shard_map/ppermute | solution.py:196
  30.1 2.2 %collective-permute-done.9.refs_7_ = bf16[4,3,16,128]{3,2,1,0:T(8,128)(2,1)S(1)} collective-permute-done((bf16[4,3,16,128]{3,2,1,0:T(8,128)(2,1)S(1)}, bf16[4,3,16,128]{3,2,1,0:T(8,128)(2,1)S(1)}, u32[]{:S(2)}, u32[]{:S(2)}) %collective-permute-start.9) | collective-permute-done | bytes 49184 | tf_op jit(solution)/shard_map/ppermute | solution.py:196
  32.2 0.2 gather_early.1.early_ref
  32.4 4.0 %all-to-all-done.late_ref = bf16[32,5,16,128]{3,2,1,0:T(8,128)(2,1)S(1)} async-done(((bf16[32,5,16,128]{3,2,1,0:T(8,128)(2,1)}), bf16[32,5,16,128]{3,2,1,0:T(8,128)(2,1)S(1)}, u32[]{:S(2)}, u32[]{:S(2)}) %all-to-all-start) | async-done | bytes 655392 | tf_op jit(solution)/shard_map/all_to_all | solution.py:200
  36.4 1.8 %interact.1 = bf16[16,16384]{1,0:T(8,128)(2,1)} custom-call(bf16[16,96,128]{2,1,0:T(8,128)(2,1)S(1)} %gather_early.1.early_ref, bf16[32,5,16,128]{3,2,1,0:T(8,128)(2,1)S(1)} %all-to-all-done.late_ref, bf16[256,256]{1,0:T(8,128)(2,1)S(1)} %convolution_convert_fusion.proj_ref, bf16[1,256]{1,0:T(2,128)(2,1)S(1)} %slice_bitcast_fusion.dense_proj_ref, ...), custom_call_target="tpu_custom_call" | custom-call | tf_op jit(solution)/shard_map/interact/pallas_call | solution.py:177
  (34 shorter events, 0.3 us)
Async XLA Ops:
  0.0 18.4 %copy-start.1 = (bf16[128,257]{0,1:T(8,128)(2,1)S(1)}, bf16[128,257]{0,1:T(8,128)(2,1)}, u32[]{:S(2)}) copy-start(bf16[128,257]{0,1:T(8,128)(2,1)} %param.12) | copy-start | bytes 197380
  0.0 18.8 %copy-start.2 = (bf16[128,257]{0,1:T(8,128)(2,1)S(1)}, bf16[128,257]{0,1:T(8,128)(2,1)}, u32[]{:S(2)}) copy-start(bf16[128,257]{0,1:T(8,128)(2,1)} %param.13) | copy-start | bytes 197380
  0.0 18.9 %copy-start.3 = (s32[256]{0:T(256)S(1)}, s32[256]{0:T(256)}, u32[]{:S(2)}) copy-start(s32[256]{0:T(256)} %param.10) | copy-start | bytes 3076
  5.7 13.5 %collective-permute-start.2 = (bf16[8,3,16,128]{3,2,1,0:T(8,128)(2,1)}, bf16[8,3,16,128]{3,2,1,0:T(8,128)(2,1)S(1)}, u32[]{:S(2)}, u32[]{:S(2)}) collective-permute-start(bf16[8,3,16,128]{3,2,1,0:T(8,128)(2,1)} %get-tuple-element.13), channel_id=1, source_target_pairs={{0,3},{1,2},{2,1},{3,0},{4,7},{5,6},{6,5},{7,4},{8,11},{9,10},{10,... | collective-permute-start | bytes 294920 | tf_op jit(solution)/shard_map/ppermute | solution.py:196
  10.8 8.5 %collective-permute-start.1 = (bf16[8,3,16,128]{3,2,1,0:T(8,128)(2,1)}, bf16[8,3,16,128]{3,2,1,0:T(8,128)(2,1)S(1)}, u32[]{:S(2)}, u32[]{:S(2)}) collective-permute-start(bf16[8,3,16,128]{3,2,1,0:T(8,128)(2,1)} %get-tuple-element.12), channel_id=1, source_target_pairs={{0,2},{1,3},{2,0},{3,1},{4,6},{5,7},{6,4},{7,5},{8,10},{9,11},{10,... | collective-permute-start | bytes 294920 | tf_op jit(solution)/shard_map/ppermute | solution.py:196
  10.8 8.5 %collective-permute-start = (bf16[8,3,16,128]{3,2,1,0:T(8,128)(2,1)}, bf16[8,3,16,128]{3,2,1,0:T(8,128)(2,1)S(1)}, u32[]{:S(2)}, u32[]{:S(2)}) collective-permute-start(bf16[8,3,16,128]{3,2,1,0:T(8,128)(2,1)} %get-tuple-element.11), channel_id=1, source_target_pairs={{0,1},{1,0},{2,3},{3,2},{4,5},{5,4},{6,7},{7,6},{8,9},{9,8},{10,11... | collective-permute-start | bytes 294920 | tf_op jit(solution)/shard_map/ppermute | solution.py:196
  11.5 24.9 %copy-start = (bf16[16,128]{1,0:T(8,128)(2,1)S(1)}, bf16[16,128]{1,0:T(8,128)(2,1)}, u32[]{:S(2)}) copy-start(bf16[16,128]{1,0:T(8,128)(2,1)} %dense_ref.1) | copy-start | bytes 12292
  11.5 24.9 %all-to-all-start = ((bf16[32,5,16,128]{3,2,1,0:T(8,128)(2,1)}), bf16[32,5,16,128]{3,2,1,0:T(8,128)(2,1)S(1)}, u32[]{:S(2)}, u32[]{:S(2)}) async-start(bf16[32,5,16,128]{3,2,1,0:T(8,128)(2,1)} %get-tuple-element.14), calls=%async_computation | async-start | bytes 1310720 | tf_op jit(solution)/shard_map/all_to_all | solution.py:200
  19.4 5.7 %collective-permute-start.3 = (bf16[4,3,16,128]{3,2,1,0:T(8,128)(2,1)S(1)}, bf16[4,3,16,128]{3,2,1,0:T(8,128)(2,1)S(1)}, u32[]{:S(2)}, u32[]{:S(2)}) collective-permute-start(bf16[4,3,16,128]{3,2,1,0:T(8,128)(2,1)S(1)} %pad_maximum_fusion.1), channel_id=1, source_target_pairs={{0,4},{4,0},{8,12},{12,8},{16,20},{20,16},{24,28},{28,24},{1,5},{5... | collective-permute-start | bytes 147464 | tf_op jit(solution)/shard_map/ppermute | solution.py:196
  21.2 6.0 %collective-permute-start.4 = (bf16[4,3,16,128]{3,2,1,0:T(8,128)(2,1)S(1)}, bf16[4,3,16,128]{3,2,1,0:T(8,128)(2,1)S(1)}, u32[]{:S(2)}, u32[]{:S(2)}) collective-permute-start(bf16[4,3,16,128]{3,2,1,0:T(8,128)(2,1)S(1)} %pad_maximum_fusion.2), channel_id=1, source_target_pairs={{0,8},{4,12},{8,0},{12,4},{16,24},{20,28},{24,16},{28,20},{1,9},{5... | collective-permute-start | bytes 147464 | tf_op jit(solution)/shard_map/ppermute | solution.py:196
  22.7 6.5 %collective-permute-start.5 = (bf16[4,3,16,128]{3,2,1,0:T(8,128)(2,1)S(1)}, bf16[4,3,16,128]{3,2,1,0:T(8,128)(2,1)S(1)}, u32[]{:S(2)}, u32[]{:S(2)}) collective-permute-start(bf16[4,3,16,128]{3,2,1,0:T(8,128)(2,1)S(1)} %pad_maximum_fusion.3), channel_id=1, source_target_pairs={{0,12},{4,8},{8,4},{12,0},{16,28},{20,24},{24,20},{28,16},{1,13},{... | collective-permute-start | bytes 147464 | tf_op jit(solution)/shard_map/ppermute | solution.py:196
  23.1 6.1 %collective-permute-start.6 = (bf16[4,3,16,128]{3,2,1,0:T(8,128)(2,1)S(1)}, bf16[4,3,16,128]{3,2,1,0:T(8,128)(2,1)S(1)}, u32[]{:S(2)}, u32[]{:S(2)}) collective-permute-start(bf16[4,3,16,128]{3,2,1,0:T(8,128)(2,1)S(1)} %pad_maximum_fusion.4), channel_id=1, source_target_pairs={{0,16},{4,20},{8,24},{12,28},{16,0},{20,4},{24,8},{28,12},{1,17},{... | collective-permute-start | bytes 147464 | tf_op jit(solution)/shard_map/ppermute | solution.py:196
  23.2 6.0 %collective-permute-start.7 = (bf16[4,3,16,128]{3,2,1,0:T(8,128)(2,1)S(1)}, bf16[4,3,16,128]{3,2,1,0:T(8,128)(2,1)S(1)}, u32[]{:S(2)}, u32[]{:S(2)}) collective-permute-start(bf16[4,3,16,128]{3,2,1,0:T(8,128)(2,1)S(1)} %pad_maximum_fusion.5), channel_id=1, source_target_pairs={{0,20},{4,16},{8,28},{12,24},{16,4},{20,0},{24,12},{28,8},{1,21},{... | collective-permute-start | bytes 147464 | tf_op jit(solution)/shard_map/ppermute | solution.py:196
  25.1 4.9 %collective-permute-start.8 = (bf16[4,3,16,128]{3,2,1,0:T(8,128)(2,1)S(1)}, bf16[4,3,16,128]{3,2,1,0:T(8,128)(2,1)S(1)}, u32[]{:S(2)}, u32[]{:S(2)}) collective-permute-start(bf16[4,3,16,128]{3,2,1,0:T(8,128)(2,1)S(1)} %pad_maximum_fusion.6), channel_id=1, source_target_pairs={{0,24},{4,28},{8,16},{12,20},{16,8},{20,12},{24,0},{28,4},{1,25},{... | collective-permute-start | bytes 147464 | tf_op jit(solution)/shard_map/ppermute | solution.py:196
  27.2 5.0 %collective-permute-start.9 = (bf16[4,3,16,128]{3,2,1,0:T(8,128)(2,1)S(1)}, bf16[4,3,16,128]{3,2,1,0:T(8,128)(2,1)S(1)}, u32[]{:S(2)}, u32[]{:S(2)}) collective-permute-start(bf16[4,3,16,128]{3,2,1,0:T(8,128)(2,1)S(1)} %pad_maximum_fusion.7), channel_id=1, source_target_pairs={{0,28},{4,24},{8,20},{12,16},{16,12},{20,8},{24,4},{28,0},{1,29},{... | collective-permute-start | bytes 147464 | tf_op jit(solution)/shard_map/ppermute | solution.py:196

commit v4 on v3

--- a/solution.py
+++ b/solution.py
@@ -13,8 +13,7 @@
 ROW_BLOCK = 256
 SAMPLE_BLOCK = 256
 VMEM_LIMIT = 24 * 1024 * 1024
-EARLY = 3
-TABLE_BLOCK = 4
+EARLY = 4
 
 
 def pool_table(ids_ref, lens_ref, table_ref, table, slot, write):
@@ -24,7 +23,7 @@
     zero = jnp.zeros((), jnp.bfloat16)
     row_iota = lax.broadcasted_iota(jnp.int32, (ROW_BLOCK, block), 0).astype(jnp.float32).astype(jnp.bfloat16)
     for at in range(0, samples, block):
-        bag = ids_ref[slot, :, at : at + block]
+        bag = ids_ref[table, :, at : at + block]
         used = lax.broadcasted_iota(jnp.int32, bag.shape, 0) < lens_ref[pl.ds(table, 1), at : at + block]
         bag = jnp.where(used, bag, -1)
         ids = [bag[j : j + 1] for j in range(bag_size)]
@@ -52,74 +51,98 @@
         write(at, block, total.T.astype(jnp.bfloat16))
 
 
-def pool_kernel(early, steps, ids_ref, lens_ref, table_ref, *refs):
-    columns = (len(refs) - 4) // 2
-    near, far = refs[:columns], refs[columns]
-    near_bufs, (far_buf, held, sems) = refs[columns + 1 : 2 * columns + 1], refs[2 * columns + 1 :]
-    step_tables = table_ref.shape[0]
+def pool_early_kernel(ids_hbm, lens_hbm, tables_hbm, *refs):
+    near, (ids_ref, lens_ref, later_ref), (table_ref, held, sems) = refs[:-6], refs[-6:-3], refs[-3:]
+    columns = len(near)
+    early = table_ref.shape[0]
     own, width = held.shape[1:]
     plane, column = lax.axis_index(PLANE), lax.axis_index(LINE)
-    copies = [pltpu.make_async_copy(near_bufs[r], near[r], sems.at[r]) for r in range(columns)]
-    for step in range(steps):
-
-        @pl.when(pl.program_id(0) == step)
-        def _(step=step):
-            for slot in range(step_tables):
-                table = step * step_tables + slot
-
-                def write(at, block, pooled):
-                    pooled = pooled.reshape(block // own, own, width)
-                    if table < early:
-                        held[at // own : (at + block) // own] = pooled
-                    else:
-                        far_buf[at // own : (at + block) // own, table - early] = pooled
-
-                pool_table(ids_ref, lens_ref, table_ref, table, slot, write)
-                if table < early:
-                    for r in range(columns):
-                        for p in range(near_bufs[r].shape[0]):
-                            device = lax.bitwise_xor(plane, p) * columns + lax.bitwise_xor(column, r)
-                            near_bufs[r][p, table] = held[device]
-                if table == early - 1:
-                    for copy in copies:
-                        copy.start()
-            if step == steps - 1:
-                last = pltpu.make_async_copy(far_buf, far, sems.at[columns])
-                last.start()
-                for copy in copies:
-                    copy.wait()
-                last.wait()
-
-
-def pool(tables, ids, lens, early, planes, columns):
+    small = [
+        pltpu.make_async_copy(ids_hbm, ids_ref, sems.at[0]),
+        pltpu.make_async_copy(lens_hbm, lens_ref, sems.at[1]),
+    ]
+    large = [
+        pltpu.make_async_copy(tables_hbm.at[slot], table_ref.at[slot], sems.at[3 + slot]) for slot in range(early)
+    ]
+    later = pltpu.make_async_copy(tables_hbm.at[pl.ds(early, later_ref.shape[0])], later_ref, sems.at[2])
+    for copy in small + large + [later]:
+        copy.start()
+    for copy in small:
+        copy.wait()
+    for slot in range(early):
+        large[slot].wait()
+
+        def write(at, block, pooled):
+            held[at // own : (at + block) // own] = pooled.reshape(block // own, own, width)
+
+        pool_table(ids_ref, lens_ref, table_ref, slot, slot, write)
+        for r in range(columns):
+            for p in range(near[r].shape[0]):
+                device = lax.bitwise_xor(plane, p) * columns + lax.bitwise_xor(column, r)
+                near[r][p, slot] = held[device]
+    later.wait()
+
+
+def pool_early(tables, ids, lens, early, planes, columns):
     tab_dev, rows, width = tables.shape
-    bag_size, samples = ids.shape[1], ids.shape[2]
-    devices = planes * columns
-    own = samples // devices
-    steps = tab_dev // TABLE_BLOCK
-    near = (planes, early, own, width)
-    far = (devices, tab_dev - early, own, width)
-    shapes = [near] * columns + [far]
+    samples = ids.shape[2]
+    own = samples // (planes * columns)
+    shapes = [jax.ShapeDtypeStruct((planes, early, own, width), jnp.bfloat16)] * columns
+    shapes += [ids, lens, jax.ShapeDtypeStruct((tab_dev - early, rows, width), jnp.bfloat16)]
     outs = pl.pallas_call(
-        functools.partial(pool_kernel, early, steps),
-        grid=(steps,),
-        in_specs=[
-            pl.BlockSpec((TABLE_BLOCK, bag_size, samples), lambda t: (t, 0, 0)),
-            pl.BlockSpec((tab_dev, samples), lambda t: (0, 0)),
-            pl.BlockSpec((TABLE_BLOCK, rows, width), lambda t: (t, 0, 0)),
+        pool_early_kernel,
+        in_specs=[pl.BlockSpec(memory_space=pltpu.HBM)] * 3,
+        out_specs=[pl.BlockSpec(memory_space=pltpu.VMEM)] * len(shapes),
+        out_shape=[jax.ShapeDtypeStruct(shape.shape, shape.dtype) for shape in shapes],
+        scratch_shapes=[
+            pltpu.VMEM((early, rows, width), jnp.bfloat16),
+            pltpu.VMEM((planes * columns, own, width), jnp.bfloat16),
+            pltpu.SemaphoreType.DMA((3 + early,)),
         ],
-        out_specs=[pl.BlockSpec(memory_space=pl.ANY)] * len(shapes),
-        out_shape=[jax.ShapeDtypeStruct(shape, jnp.bfloat16) for shape in shapes],
-        scratch_shapes=[pltpu.VMEM(shape, jnp.bfloat16) for shape in shapes]
-        + [pltpu.VMEM((devices, own, width), jnp.bfloat16), pltpu.SemaphoreType.DMA((len(shapes),))],
-        cost_estimate=pl.CostEstimate(
-            flops=2 * tab_dev * rows * samples * width,
-            bytes_accessed=2 * tab_dev * (rows + samples) * width,
-            transcendentals=0,
-        ),
-        name="pool",
+        compiler_params=pltpu.CompilerParams(vmem_limit_bytes=VMEM_LIMIT),
+        cost_estimate=pool_cost(early, samples, rows, width),
+        name="pool_early",
+    )(*[pltpu.with_memory_space_constraint(x, pltpu.HBM) for x in (ids, lens, tables)])
+    return outs[:columns], outs[columns:]
+
+
+def pool_late_kernel(early, ids_ref, lens_ref, table_ref, far, far_buf, sems):
+    own = far.shape[2]
+    copies = []
+    for slot in range(table_ref.shape[0]):
+
+        def write(at, block, pooled):
+            far_buf[at // own : (at + block) // own, slot] = pooled.reshape(block // own, own, pooled.shape[1])
+
+        pool_table(ids_ref, lens_ref, table_ref, early + slot, slot, write)
+        copies.append(pltpu.make_async_copy(far_buf.at[:, slot], far.at[:, slot], sems.at[slot]))
+        copies[-1].start()
+    for copy in copies:
+        copy.wait()
+
+
+def pool_late(tables, ids, lens, early, devices):
+    late, rows, width = tables.shape
+    samples = ids.shape[2]
+    far = (devices, late, samples // devices, width)
+    return pl.pallas_call(
+        functools.partial(pool_late_kernel, early),
+        in_specs=[pl.BlockSpec(memory_space=pltpu.VMEM)] * 3,
+        out_specs=pl.BlockSpec(memory_space=pl.ANY),
+        out_shape=jax.ShapeDtypeStruct(far, jnp.bfloat16),
+        scratch_shapes=[pltpu.VMEM(far, jnp.bfloat16), pltpu.SemaphoreType.DMA((late,))],
+        compiler_params=pltpu.CompilerParams(vmem_limit_bytes=VMEM_LIMIT),
+        cost_estimate=pool_cost(late, samples, rows, width),
+        name="pool_late",
     )(ids, lens, tables)
-    return outs[:-1], outs[-1]
+
+
+def pool_cost(tables, samples, rows, width):
+    return pl.CostEstimate(
+        flops=2 * tables * rows * samples * width,
+        bytes_accessed=2 * tables * (rows + samples) * width,
+        transcendentals=0,
+    )
 
 
 def by_sample(blocks):
@@ -195,8 +218,9 @@
     def swap(x, axis, size, distance):
         return lax.ppermute(x, axis, [(i, i ^ distance) for i in range(size)])
 
-    near, blocks = pool(tables, indices.transpose(0, 2, 1), lengths, early, planes, columns)
+    near, (ids, lens, later) = pool_early(tables, indices.transpose(0, 2, 1), lengths, early, planes, columns)
     arrived = {r: swap(near[r], LINE, columns, r) for r in range(1, columns)}
+    blocks = pool_late(later, ids, lens, early, devices)
     late = lax.all_to_all(blocks, AXES, split_axis=0, concat_axis=0, tiled=True)
     stacked = [jnp.stack([near[0][p]] + [arrived[r][p] for r in range(1, columns)]) for p in range(planes)]
     pieces = [stacked[0]] + [swap(stacked[p], PLANE, planes, p) for p in range(1, planes)]

time: 38.4 us -> 38.2 us (level)
  the two profiles are of different devices: /device:TPU:0 before, /device:TPU:16 now
where the time goes in v4:
time: 38.2 us; the launch traced here: 37.9 us
  starting transfers between devices  17.2 us (45%)
  waiting for transfers between devices  11.5 us (30%)
  Pallas kernels  8.03 us (21%)
    ppermute x10, waiting for transfers between devices, swap(): return lax.ppermute(x, axis, [(i, i ^ distance) for i in range(size)])  11.5 us
    ppermute x10, starting transfers between devices, swap(): return lax.ppermute(x, axis, [(i, i ^ distance) for i in range(size)])  10.3 us
    all_to_all x1, starting transfers between devices, shards(): late = lax.all_to_all(blocks, AXES, split_axis=0, concat_axis=0, tiled=True)  6.86 us
    pallas_call x1, Pallas kernels, pool_early(): pl.pallas_call(pool_early_kernel, in_specs=[pl.BlockSpec(memory_space=plt...  3.7 us
    pallas_call x1, Pallas kernels, pool_late(): pl.pallas_call(functools.partial(pool_late_kernel, early), in_specs=[pl.B...  2.39 us
    pallas_call x1, Pallas kernels, interact(): pl.pallas_call(interact_kernel, in_specs=[vmem] * 5, out_specs=vmem, out_...  1.77 us
  transfers between devices with their start and end apart: 11, of which 5 were waited for; matrix products, arithmetic and copies ran while one was open for 2% of the time, Pallas kernels for 7%

profile of v4, /device:TPU:16, one launch (start us, length us, event | category | flops | bytes accessed | tf_op | source)
XLA Modules:
  0.0 37.9 jit_solution(17774348541918390123)
XLA Ops:
  0.0 3.7 %pool_early.1 = (bf16[8,4,16,128]{3,2,1,0:T(8,128)(2,1)S(1)}, bf16[8,4,16,128]{3,2,1,0:T(8,128)(2,1)S(1)}, bf16[8,4,16,128]{3,2,1,0:T(8,128)(2,1)S(1)}, bf16[8,4...) custom-call(s32[8,4,512]{2,1,0:T(4,128)} %bitcast.3, ...), custom_call_target="tpu_custom_call" | custom-call | flops 536870912 | bytes 1572864 | tf_op jit(solution)/shard_map/pool_early/pallas_call | solution.py:92
  3.7 1.7 %collective-permute-start = (bf16[8,4,16,128]{3,2,1,0:T(8,128)(2,1)S(1)}, bf16[8,4,16,128]{3,2,1,0:T(8,128)(2,1)S(1)}, u32[]{:S(2)}, u32[]{:S(2)}) collective-permute-start(bf16[8,4,16,128]{3,2,1,0:T(8,128)(2,1)S(1)} %get-tuple-element.13), channel_id=1, source_target_pairs={{0,1},{1,0},{2,3},{3,2},{4,5},{5,4},{6,7},{7,6},{8,9},{9,8},{10,11... | collective-permute-start | bytes 393224 | tf_op jit(solution)/shard_map/ppermute | solution.py:219
  5.4 0.3 collective-permute-start.1
  5.7 1.6 %collective-permute-start.2 = (bf16[8,4,16,128]{3,2,1,0:T(8,128)(2,1)S(1)}, bf16[8,4,16,128]{3,2,1,0:T(8,128)(2,1)S(1)}, u32[]{:S(2)}, u32[]{:S(2)}) collective-permute-start(bf16[8,4,16,128]{3,2,1,0:T(8,128)(2,1)S(1)} %get-tuple-element.15), channel_id=1, source_target_pairs={{0,3},{1,2},{2,1},{3,0},{4,7},{5,6},{6,5},{7,4},{8,11},{9,10},{10,... | collective-permute-start | bytes 393224 | tf_op jit(solution)/shard_map/ppermute | solution.py:219
  7.3 2.4 %pool_late.1 = bf16[32,4,16,128]{3,2,1,0:T(8,128)(2,1)} custom-call(s32[8,4,512]{2,1,0:T(4,128)S(1)} %get-tuple-element.16.ids_ref, s32[8,512]{1,0:T(8,128)S(1)} %get-tuple-element.17.lens_ref, bf16[4,1024,128]{2,1,0:T(8,128)(2,1)S(1)} %get-tuple-element.18.table_ref), custom_call_target="tpu_custom_call" | custom-call | flops 536870912 | bytes 1572864 | tf_op jit(solution)/shard_map/pool_late/pallas_call | solution.py:128
  9.7 6.9 %all-to-all-start = ((bf16[32,4,16,128]{3,2,1,0:T(8,128)(2,1)}), bf16[32,4,16,128]{3,2,1,0:T(8,128)(2,1)S(1)}, u32[]{:S(2)}, u32[]{:S(2)}) async-start(bf16[32,4,16,128]{3,2,1,0:T(8,128)(2,1)} %pool_late.1), calls=%async_computation | async-start | bytes 1048576 | tf_op jit(solution)/shard_map/all_to_all | solution.py:224
  16.7 0.1 iota_add_fusion
  16.7 0.1 add.28
  16.9 0.1 broadcast_add_fusion
  16.9 0.1 add.31
  17.1 0.3 convolution_convert_fusion.proj_ref
  17.5 3.7 %collective-permute-done.2 = bf16[8,4,16,128]{3,2,1,0:T(8,128)(2,1)S(1)} collective-permute-done((bf16[8,4,16,128]{3,2,1,0:T(8,128)(2,1)S(1)}, bf16[8,4,16,128]{3,2,1,0:T(8,128)(2,1)S(1)}, u32[]{:S(2)}, u32[]{:S(2)}) %collective-permute-start.2) | collective-permute-done | bytes 131104 | tf_op jit(solution)/shard_map/ppermute | solution.py:219
  21.2 0.1 collective-permute-start.9
  21.3 2.8 %collective-permute-start.8 = (bf16[4,4,16,128]{3,2,1,0:T(8,128)(2,1)S(1)}, bf16[4,4,16,128]{3,2,1,0:T(8,128)(2,1)S(1)}, u32[]{:S(2)}, u32[]{:S(2)}) collective-permute-start(bf16[4,4,16,128]{3,2,1,0:T(8,128)(2,1)S(1)} %pad_maximum_fusion.6), channel_id=1, source_target_pairs={{0,24},{4,28},{8,16},{12,20},{16,8},{20,12},{24,0},{28,4},{1,25},{... | collective-permute-start | bytes 196616 | tf_op jit(solution)/shard_map/ppermute | solution.py:219
  24.1 0.3 collective-permute-start.7
  24.4 0.4 %collective-permute-start.6 = (bf16[4,4,16,128]{3,2,1,0:T(8,128)(2,1)S(1)}, bf16[4,4,16,128]{3,2,1,0:T(8,128)(2,1)S(1)}, u32[]{:S(2)}, u32[]{:S(2)}) collective-permute-start(bf16[4,4,16,128]{3,2,1,0:T(8,128)(2,1)S(1)} %pad_maximum_fusion.4), channel_id=1, source_target_pairs={{0,16},{4,20},{8,24},{12,28},{16,0},{20,4},{24,8},{28,12},{1,17},{... | collective-permute-start | bytes 196616 | tf_op jit(solution)/shard_map/ppermute | solution.py:219
  24.8 2.8 %collective-permute-start.5 = (bf16[4,4,16,128]{3,2,1,0:T(8,128)(2,1)S(1)}, bf16[4,4,16,128]{3,2,1,0:T(8,128)(2,1)S(1)}, u32[]{:S(2)}, u32[]{:S(2)}) collective-permute-start(bf16[4,4,16,128]{3,2,1,0:T(8,128)(2,1)S(1)} %pad_maximum_fusion.3), channel_id=1, source_target_pairs={{0,12},{4,8},{8,4},{12,0},{16,28},{20,24},{24,20},{28,16},{1,13},{... | collective-permute-start | bytes 196616 | tf_op jit(solution)/shard_map/ppermute | solution.py:219
  27.6 0.4 %collective-permute-start.4 = (bf16[4,4,16,128]{3,2,1,0:T(8,128)(2,1)S(1)}, bf16[4,4,16,128]{3,2,1,0:T(8,128)(2,1)S(1)}, u32[]{:S(2)}, u32[]{:S(2)}) collective-permute-start(bf16[4,4,16,128]{3,2,1,0:T(8,128)(2,1)S(1)} %pad_maximum_fusion.2), channel_id=1, source_target_pairs={{0,8},{4,12},{8,0},{12,4},{16,24},{20,28},{24,16},{28,20},{1,9},{5... | collective-permute-start | bytes 196616 | tf_op jit(solution)/shard_map/ppermute | solution.py:219
  28.1 3.3 %collective-permute-done.8.refs_6_ = bf16[4,4,16,128]{3,2,1,0:T(8,128)(2,1)S(1)} collective-permute-done((bf16[4,4,16,128]{3,2,1,0:T(8,128)(2,1)S(1)}, bf16[4,4,16,128]{3,2,1,0:T(8,128)(2,1)S(1)}, u32[]{:S(2)}, u32[]{:S(2)}) %collective-permute-start.8) | collective-permute-done | bytes 65568 | tf_op jit(solution)/shard_map/ppermute | solution.py:219
  31.4 0.3 collective-permute-done.5.refs_3_
  31.6 1.5 %collective-permute-done.4.refs_2_ = bf16[4,4,16,128]{3,2,1,0:T(8,128)(2,1)S(1)} collective-permute-done((bf16[4,4,16,128]{3,2,1,0:T(8,128)(2,1)S(1)}, bf16[4,4,16,128]{3,2,1,0:T(8,128)(2,1)S(1)}, u32[]{:S(2)}, u32[]{:S(2)}) %collective-permute-start.4) | collective-permute-done | bytes 65568 | tf_op jit(solution)/shard_map/ppermute | solution.py:219
  33.1 2.8 %collective-permute-done.3.refs_1_ = bf16[4,4,16,128]{3,2,1,0:T(8,128)(2,1)S(1)} collective-permute-done((bf16[4,4,16,128]{3,2,1,0:T(8,128)(2,1)S(1)}, bf16[4,4,16,128]{3,2,1,0:T(8,128)(2,1)S(1)}, u32[]{:S(2)}, u32[]{:S(2)}) %collective-permute-start.3) | collective-permute-done | bytes 65568 | tf_op jit(solution)/shard_map/ppermute | solution.py:219
  35.9 0.2 gather_early.1.early_ref
  36.1 1.8 %interact.1 = bf16[16,16384]{1,0:T(8,128)(2,1)} custom-call(bf16[16,128,128]{2,1,0:T(8,128)(2,1)S(1)} %gather_early.1.early_ref, bf16[32,4,16,128]{3,2,1,0:T(8,128)(2,1)S(1)} %all-to-all-done.late_ref, bf16[256,256]{1,0:T(8,128)(2,1)S(1)} %convolution_convert_fusion.proj_ref, bf16[1,256]{1,0:T(2,128)(2,1)S(1)} %slice_bitcast_fusion.dense_proj_ref, ...), custom_call_target="tpu_custom_call" | custom-call | tf_op jit(solution)/shard_map/interact/pallas_call | solution.py:200
  (35 shorter events, 0.3 us)
Async XLA Ops:
  3.7 13.3 %copy-start.1 = (bf16[128,257]{0,1:T(8,128)(2,1)S(1)}, bf16[128,257]{0,1:T(8,128)(2,1)}, u32[]{:S(2)}) copy-start(bf16[128,257]{0,1:T(8,128)(2,1)} %param.12) | copy-start | bytes 197380
  3.7 13.4 %copy-start.2 = (bf16[128,257]{0,1:T(8,128)(2,1)S(1)}, bf16[128,257]{0,1:T(8,128)(2,1)}, u32[]{:S(2)}) copy-start(bf16[128,257]{0,1:T(8,128)(2,1)} %param.13) | copy-start | bytes 197380
  3.7 13.4 %copy-start.3 = (s32[256]{0:T(256)S(1)}, s32[256]{0:T(256)}, u32[]{:S(2)}) copy-start(s32[256]{0:T(256)} %param.10) | copy-start | bytes 3076
  3.7 13.7 %collective-permute-start = (bf16[8,4,16,128]{3,2,1,0:T(8,128)(2,1)S(1)}, bf16[8,4,16,128]{3,2,1,0:T(8,128)(2,1)S(1)}, u32[]{:S(2)}, u32[]{:S(2)}) collective-permute-start(bf16[8,4,16,128]{3,2,1,0:T(8,128)(2,1)S(1)} %get-tuple-element.13), channel_id=1, source_target_pairs={{0,1},{1,0},{2,3},{3,2},{4,5},{5,4},{6,7},{7,6},{8,9},{9,8},{10,11... | collective-permute-start | bytes 393224 | tf_op jit(solution)/shard_map/ppermute | solution.py:219
  5.4 12.1 %collective-permute-start.1 = (bf16[8,4,16,128]{3,2,1,0:T(8,128)(2,1)S(1)}, bf16[8,4,16,128]{3,2,1,0:T(8,128)(2,1)S(1)}, u32[]{:S(2)}, u32[]{:S(2)}) collective-permute-start(bf16[8,4,16,128]{3,2,1,0:T(8,128)(2,1)S(1)} %get-tuple-element.14), channel_id=1, source_target_pairs={{0,2},{1,3},{2,0},{3,1},{4,6},{5,7},{6,4},{7,5},{8,10},{9,11},{10,... | collective-permute-start | bytes 393224 | tf_op jit(solution)/shard_map/ppermute | solution.py:219
  5.7 15.4 %collective-permute-start.2 = (bf16[8,4,16,128]{3,2,1,0:T(8,128)(2,1)S(1)}, bf16[8,4,16,128]{3,2,1,0:T(8,128)(2,1)S(1)}, u32[]{:S(2)}, u32[]{:S(2)}) collective-permute-start(bf16[8,4,16,128]{3,2,1,0:T(8,128)(2,1)S(1)} %get-tuple-element.15), channel_id=1, source_target_pairs={{0,3},{1,2},{2,1},{3,0},{4,7},{5,6},{6,5},{7,4},{8,11},{9,10},{10,... | collective-permute-start | bytes 393224 | tf_op jit(solution)/shard_map/ppermute | solution.py:219
  9.7 26.4 %all-to-all-start = ((bf16[32,4,16,128]{3,2,1,0:T(8,128)(2,1)}), bf16[32,4,16,128]{3,2,1,0:T(8,128)(2,1)S(1)}, u32[]{:S(2)}, u32[]{:S(2)}) async-start(bf16[32,4,16,128]{3,2,1,0:T(8,128)(2,1)} %pool_late.1), calls=%async_computation | async-start | bytes 1048576 | tf_op jit(solution)/shard_map/all_to_all | solution.py:224
  16.6 19.6 %copy-start = (bf16[16,128]{1,0:T(8,128)(2,1)S(1)}, bf16[16,128]{1,0:T(8,128)(2,1)}, u32[]{:S(2)}) copy-start(bf16[16,128]{1,0:T(8,128)(2,1)} %dense_ref.1) | copy-start | bytes 12292
  21.2 6.4 %collective-permute-start.9 = (bf16[4,4,16,128]{3,2,1,0:T(8,128)(2,1)S(1)}, bf16[4,4,16,128]{3,2,1,0:T(8,128)(2,1)S(1)}, u32[]{:S(2)}, u32[]{:S(2)}) collective-permute-start(bf16[4,4,16,128]{3,2,1,0:T(8,128)(2,1)S(1)} %pad_maximum_fusion.7), channel_id=1, source_target_pairs={{0,28},{4,24},{8,20},{12,16},{16,12},{20,8},{24,4},{28,0},{1,29},{... | collective-permute-start | bytes 196616 | tf_op jit(solution)/shard_map/ppermute | solution.py:219
  21.3 10.0 %collective-permute-start.8 = (bf16[4,4,16,128]{3,2,1,0:T(8,128)(2,1)S(1)}, bf16[4,4,16,128]{3,2,1,0:T(8,128)(2,1)S(1)}, u32[]{:S(2)}, u32[]{:S(2)}) collective-permute-start(bf16[4,4,16,128]{3,2,1,0:T(8,128)(2,1)S(1)} %pad_maximum_fusion.6), channel_id=1, source_target_pairs={{0,24},{4,28},{8,16},{12,20},{16,8},{20,12},{24,0},{28,4},{1,25},{... | collective-permute-start | bytes 196616 | tf_op jit(solution)/shard_map/ppermute | solution.py:219
  24.1 7.2 %collective-permute-start.7 = (bf16[4,4,16,128]{3,2,1,0:T(8,128)(2,1)S(1)}, bf16[4,4,16,128]{3,2,1,0:T(8,128)(2,1)S(1)}, u32[]{:S(2)}, u32[]{:S(2)}) collective-permute-start(bf16[4,4,16,128]{3,2,1,0:T(8,128)(2,1)S(1)} %pad_maximum_fusion.5), channel_id=1, source_target_pairs={{0,20},{4,16},{8,28},{12,24},{16,4},{20,0},{24,12},{28,8},{1,21},{... | collective-permute-start | bytes 196616 | tf_op jit(solution)/shard_map/ppermute | solution.py:219
  24.4 6.9 %collective-permute-start.6 = (bf16[4,4,16,128]{3,2,1,0:T(8,128)(2,1)S(1)}, bf16[4,4,16,128]{3,2,1,0:T(8,128)(2,1)S(1)}, u32[]{:S(2)}, u32[]{:S(2)}) collective-permute-start(bf16[4,4,16,128]{3,2,1,0:T(8,128)(2,1)S(1)} %pad_maximum_fusion.4), channel_id=1, source_target_pairs={{0,16},{4,20},{8,24},{12,28},{16,0},{20,4},{24,8},{28,12},{1,17},{... | collective-permute-start | bytes 196616 | tf_op jit(solution)/shard_map/ppermute | solution.py:219
  24.8 6.8 %collective-permute-start.5 = (bf16[4,4,16,128]{3,2,1,0:T(8,128)(2,1)S(1)}, bf16[4,4,16,128]{3,2,1,0:T(8,128)(2,1)S(1)}, u32[]{:S(2)}, u32[]{:S(2)}) collective-permute-start(bf16[4,4,16,128]{3,2,1,0:T(8,128)(2,1)S(1)} %pad_maximum_fusion.3), channel_id=1, source_target_pairs={{0,12},{4,8},{8,4},{12,0},{16,28},{20,24},{24,20},{28,16},{1,13},{... | collective-permute-start | bytes 196616 | tf_op jit(solution)/shard_map/ppermute | solution.py:219
  27.6 5.5 %collective-permute-start.4 = (bf16[4,4,16,128]{3,2,1,0:T(8,128)(2,1)S(1)}, bf16[4,4,16,128]{3,2,1,0:T(8,128)(2,1)S(1)}, u32[]{:S(2)}, u32[]{:S(2)}) collective-permute-start(bf16[4,4,16,128]{3,2,1,0:T(8,128)(2,1)S(1)} %pad_maximum_fusion.2), channel_id=1, source_target_pairs={{0,8},{4,12},{8,0},{12,4},{16,24},{20,28},{24,16},{28,20},{1,9},{5... | collective-permute-start | bytes 196616 | tf_op jit(solution)/shard_map/ppermute | solution.py:219
  31.3 4.6 %collective-permute-start.3 = (bf16[4,4,16,128]{3,2,1,0:T(8,128)(2,1)S(1)}, bf16[4,4,16,128]{3,2,1,0:T(8,128)(2,1)S(1)}, u32[]{:S(2)}, u32[]{:S(2)}) collective-permute-start(bf16[4,4,16,128]{3,2,1,0:T(8,128)(2,1)S(1)} %pad_maximum_fusion.1), channel_id=1, source_target_pairs={{0,4},{4,0},{8,12},{12,8},{16,20},{20,16},{24,28},{28,24},{1,5},{5... | collective-permute-start | bytes 196616 | tf_op jit(solution)/shard_map/ppermute | solution.py:219

commit v5 on v4

--- a/solution.py
+++ b/solution.py
@@ -7,55 +7,68 @@
 from jax.experimental.pallas import tpu as pltpu
 from jax.sharding import PartitionSpec as P
 
+
 AXES = ("hst", "row", "col")
 PLANE = ("hst", "row")
 LINE = "col"
 ROW_BLOCK = 256
+GROUP = 64
 SAMPLE_BLOCK = 256
 VMEM_LIMIT = 24 * 1024 * 1024
 EARLY = 4
-
-
-def pool_table(ids_ref, lens_ref, table_ref, table, slot, write):
-    bag_size, samples = ids_ref.shape[1:]
-    rows = table_ref.shape[1]
+AHEAD = 1
+
+
+def count_ids(ids_ref, lens_ref, table, at, block, rows):
+    bag_size = ids_ref.shape[1]
+    bag = ids_ref[table, :, at : at + block]
+    used = lax.broadcasted_iota(jnp.int32, bag.shape, 0) < lens_ref[pl.ds(table, 1), at : at + block]
+    low = lax.bitwise_and(bag, GROUP - 1).astype(jnp.int16)
+    group = jnp.where(used, lax.shift_right_logical(bag, GROUP.bit_length() - 1), -1).astype(jnp.int16)
+    row_iota = lax.broadcasted_iota(jnp.int32, (GROUP, block), 0).astype(jnp.int16)
+    one, zero = jnp.ones((), jnp.bfloat16), jnp.zeros((), jnp.bfloat16)
+    hits = [jnp.where(low[j : j + 1] == row_iota, one, zero) for j in range(bag_size)]
+    groups = [jnp.broadcast_to(group[j : j + 1], (GROUP, block)) for j in range(bag_size)]
+    for later in range(1, bag_size):
+        for earlier in range(later):
+            same = groups[earlier] == groups[later]
+            hits[earlier] = hits[earlier] + jnp.where(same, hits[later], zero)
+            groups[later] = jnp.where(same, jnp.int16(-1), groups[later])
+    counts = []
+    for start in range(0, rows, ROW_BLOCK):
+        parts = []
+        for g in range(start // GROUP, (start + ROW_BLOCK) // GROUP):
+            total = zero
+            for j in range(bag_size):
+                total = jnp.where(groups[j] == jnp.int16(g), hits[j], total)
+            parts.append(total)
+        counts.append(jnp.concatenate(parts, 0))
+    return counts
+
+
+def pool_block(table_ref, slot, counts):
+    total = None
+    for block, count in enumerate(counts):
+        part = lax.dot_general(
+            table_ref[slot, block * ROW_BLOCK : (block + 1) * ROW_BLOCK, :],
+            count,
+            (((0,), (0,)), ((), ())),
+            preferred_element_type=jnp.float32,
+        )
+        total = part if total is None else total + part
+    return total.T.astype(jnp.bfloat16)
+
+
+def sample_blocks(samples):
     block = min(SAMPLE_BLOCK, samples)
-    zero = jnp.zeros((), jnp.bfloat16)
-    row_iota = lax.broadcasted_iota(jnp.int32, (ROW_BLOCK, block), 0).astype(jnp.float32).astype(jnp.bfloat16)
-    for at in range(0, samples, block):
-        bag = ids_ref[table, :, at : at + block]
-        used = lax.broadcasted_iota(jnp.int32, bag.shape, 0) < lens_ref[pl.ds(table, 1), at : at + block]
-        bag = jnp.where(used, bag, -1)
-        ids = [bag[j : j + 1] for j in range(bag_size)]
-        times = [jnp.ones_like(ids[0]) for _ in range(bag_size)]
-        for later in range(1, bag_size):
-            for earlier in range(later):
-                same = ids[earlier] == ids[later]
-                times[earlier] = times[earlier] + jnp.where(same, times[later], 0)
-                ids[later] = jnp.where(same, -1, ids[later])
-                times[later] = jnp.where(same, 0, times[later])
-        times = [t.astype(jnp.float32).astype(jnp.bfloat16) for t in times]
-        total = None
-        for start in range(0, rows, ROW_BLOCK):
-            counts = zero
-            for j in range(bag_size):
-                here = (ids[j] - start).astype(jnp.float32).astype(jnp.bfloat16)
-                counts = jnp.where(here == row_iota, times[j], counts)
-            part = lax.dot_general(
-                table_ref[slot, start : start + ROW_BLOCK, :],
-                counts,
-                (((0,), (0,)), ((), ())),
-                preferred_element_type=jnp.float32,
-            )
-            total = part if total is None else total + part
-        write(at, block, total.T.astype(jnp.bfloat16))
+    return block, range(0, samples, block)
 
 
 def pool_early_kernel(ids_hbm, lens_hbm, tables_hbm, *refs):
     near, (ids_ref, lens_ref, later_ref), (table_ref, held, sems) = refs[:-6], refs[-6:-3], refs[-3:]
     columns = len(near)
     early = table_ref.shape[0]
-    own, width = held.shape[1:]
+    own, width = held.shape[2:]
     plane, column = lax.axis_index(PLANE), lax.axis_index(LINE)
     small = [
         pltpu.make_async_copy(ids_hbm, ids_ref, sems.at[0]),
@@ -69,17 +82,18 @@
         copy.start()
     for copy in small:
         copy.wait()
+    block, starts = sample_blocks(ids_ref.shape[2])
+    rows = table_ref.shape[1]
+    ahead = [count_ids(ids_ref, lens_ref, 0, at, block, rows) for at in starts[:AHEAD]]
     for slot in range(early):
         large[slot].wait()
-
-        def write(at, block, pooled):
-            held[at // own : (at + block) // own] = pooled.reshape(block // own, own, width)
-
-        pool_table(ids_ref, lens_ref, table_ref, slot, slot, write)
-        for r in range(columns):
-            for p in range(near[r].shape[0]):
-                device = lax.bitwise_xor(plane, p) * columns + lax.bitwise_xor(column, r)
-                near[r][p, slot] = held[device]
+        for n, at in enumerate(starts):
+            counts = ahead[n] if slot == 0 and n < AHEAD else count_ids(ids_ref, lens_ref, slot, at, block, rows)
+            pooled = pool_block(table_ref, slot, counts)
+            held[at // own : (at + block) // own, slot] = pooled.reshape(block // own, own, width)
+    for r in range(columns):
+        for p in range(near[r].shape[0]):
+            near[r][p] = held[lax.bitwise_xor(plane, p) * columns + lax.bitwise_xor(column, r)]
     later.wait()
 
 
@@ -96,7 +110,7 @@
         out_shape=[jax.ShapeDtypeStruct(shape.shape, shape.dtype) for shape in shapes],
         scratch_shapes=[
             pltpu.VMEM((early, rows, width), jnp.bfloat16),
-            pltpu.VMEM((planes * columns, own, width), jnp.bfloat16),
+            pltpu.VMEM((planes * columns, early, own, width), jnp.bfloat16),
             pltpu.SemaphoreType.DMA((3 + early,)),
         ],
         compiler_params=pltpu.CompilerParams(vmem_limit_bytes=VMEM_LIMIT),
@@ -109,12 +123,12 @@
 def pool_late_kernel(early, ids_ref, lens_ref, table_ref, far, far_buf, sems):
     own = far.shape[2]
     copies = []
+    block, starts = sample_blocks(ids_ref.shape[2])
     for slot in range(table_ref.shape[0]):
-
-        def write(at, block, pooled):
+        for at in starts:
+            counts = count_ids(ids_ref, lens_ref, early + slot, at, block, table_ref.shape[1])
+            pooled = pool_block(table_ref, slot, counts)
             far_buf[at // own : (at + block) // own, slot] = pooled.reshape(block // own, own, pooled.shape[1])
-
-        pool_table(ids_ref, lens_ref, table_ref, early + slot, slot, write)
         copies.append(pltpu.make_async_copy(far_buf.at[:, slot], far.at[:, slot], sems.at[slot]))
         copies[-1].start()
     for copy in copies:
@@ -219,7 +233,9 @@
         return lax.ppermute(x, axis, [(i, i ^ distance) for i in range(size)])
 
     near, (ids, lens, later) = pool_early(tables, indices.transpose(0, 2, 1), lengths, early, planes, columns)
-    arrived = {r: swap(near[r], LINE, columns, r) for r in range(1, columns)}
+    arrived = {}
+    for r in range(1, columns):
+        arrived[r] = swap(near[r], LINE, columns, r)
     blocks = pool_late(later, ids, lens, early, devices)
     late = lax.all_to_all(blocks, AXES, split_axis=0, concat_axis=0, tiled=True)
     stacked = [jnp.stack([near[0][p]] + [arrived[r][p] for r in range(1, columns)]) for p in range(planes)]

time: 38.2 us -> 37.2 us (0.974)
  the two profiles are of different devices: /device:TPU:16 before, /device:TPU:17 now
where the time goes in v5:
time: 37.2 us; the launch traced here: 36.9 us
  starting transfers between devices  23.3 us (63%)
  Pallas kernels  6.99 us (19%)
  waiting for transfers between devices  5.46 us (15%)
    ppermute x10, starting transfers between devices, swap(): return lax.ppermute(x, axis, [(i, i ^ distance) for i in range(size)])  15.3 us
    all_to_all x1, starting transfers between devices, shards(): late = lax.all_to_all(blocks, AXES, split_axis=0, concat_axis=0, tiled=True)  7.97 us
    ppermute x10, waiting for transfers between devices, swap(): return lax.ppermute(x, axis, [(i, i ^ distance) for i in range(size)])  5.46 us
    pallas_call x1, Pallas kernels, pool_early(): pl.pallas_call(pool_early_kernel, in_specs=[pl.BlockSpec(memory_space=plt...  3.04 us
    pallas_call x1, Pallas kernels, pool_late(): pl.pallas_call(functools.partial(pool_late_kernel, early), in_specs=[pl.B...  2.02 us
    pallas_call x1, Pallas kernels, interact(): pl.pallas_call(interact_kernel, in_specs=[vmem] * 5, out_specs=vmem, out_...  1.76 us
  transfers between devices with their start and end apart: 11, of which 5 were waited for; matrix products, arithmetic and copies ran while one was open for 2% of the time, Pallas kernels for 6%

profile of v5, /device:TPU:17, one launch (start us, length us, event | category | flops | bytes accessed | tf_op | source)
XLA Modules:
  0.0 36.9 jit_solution(16971341252770971172)
XLA Ops:
  0.0 3.0 %pool_early.1 = (bf16[8,4,16,128]{3,2,1,0:T(8,128)(2,1)S(1)}, bf16[8,4,16,128]{3,2,1,0:T(8,128)(2,1)S(1)}, bf16[8,4,16,128]{3,2,1,0:T(8,128)(2,1)S(1)}, bf16[8,4...) custom-call(s32[8,4,512]{2,1,0:T(4,128)} %bitcast.3, ...), custom_call_target="tpu_custom_call" | custom-call | flops 536870912 | bytes 1572864 | tf_op jit(solution)/shard_map/pool_early/pallas_call | solution.py:106
  3.1 1.4 %collective-permute-start = (bf16[8,4,16,128]{3,2,1,0:T(8,128)(2,1)S(1)}, bf16[8,4,16,128]{3,2,1,0:T(8,128)(2,1)S(1)}, u32[]{:S(2)}, u32[]{:S(2)}) collective-permute-start(bf16[8,4,16,128]{3,2,1,0:T(8,128)(2,1)S(1)} %get-tuple-element.13), channel_id=1, source_target_pairs={{0,1},{1,0},{2,3},{3,2},{4,5},{5,4},{6,7},{7,6},{8,9},{9,8},{10,11... | collective-permute-start | bytes 393224 | tf_op jit(solution)/shard_map/ppermute | solution.py:233
  4.5 0.1 collective-permute-start.1
  4.5 1.3 %collective-permute-start.2 = (bf16[8,4,16,128]{3,2,1,0:T(8,128)(2,1)S(1)}, bf16[8,4,16,128]{3,2,1,0:T(8,128)(2,1)S(1)}, u32[]{:S(2)}, u32[]{:S(2)}) collective-permute-start(bf16[8,4,16,128]{3,2,1,0:T(8,128)(2,1)S(1)} %get-tuple-element.15), channel_id=1, source_target_pairs={{0,3},{1,2},{2,1},{3,0},{4,7},{5,6},{6,5},{7,4},{8,11},{9,10},{10,... | collective-permute-start | bytes 393224 | tf_op jit(solution)/shard_map/ppermute | solution.py:233
  5.8 2.0 %pool_late.1 = bf16[32,4,16,128]{3,2,1,0:T(8,128)(2,1)} custom-call(s32[8,4,512]{2,1,0:T(4,128)S(1)} %get-tuple-element.16.ids_ref, s32[8,512]{1,0:T(8,128)S(1)} %get-tuple-element.17.lens_ref, bf16[4,1024,128]{2,1,0:T(8,128)(2,1)S(1)} %get-tuple-element.18.table_ref), custom_call_target="tpu_custom_call" | custom-call | flops 536870912 | bytes 1572864 | tf_op jit(solution)/shard_map/pool_late/pallas_call | solution.py:142
  7.8 8.0 %all-to-all-start = ((bf16[32,4,16,128]{3,2,1,0:T(8,128)(2,1)}), bf16[32,4,16,128]{3,2,1,0:T(8,128)(2,1)S(1)}, u32[]{:S(2)}, u32[]{:S(2)}) async-start(bf16[32,4,16,128]{3,2,1,0:T(8,128)(2,1)} %pool_late.1), calls=%async_computation | async-start | bytes 1048576 | tf_op jit(solution)/shard_map/all_to_all | solution.py:240
  15.9 0.1 iota_add_fusion
  16.0 0.1 add.28
  16.1 0.1 broadcast_add_fusion
  16.2 0.1 add.31
  16.4 0.3 convolution_convert_fusion.proj_ref
  16.7 0.4 %collective-permute-done.2 = bf16[8,4,16,128]{3,2,1,0:T(8,128)(2,1)S(1)} collective-permute-done((bf16[8,4,16,128]{3,2,1,0:T(8,128)(2,1)S(1)}, bf16[8,4,16,128]{3,2,1,0:T(8,128)(2,1)S(1)}, u32[]{:S(2)}, u32[]{:S(2)}) %collective-permute-start.2) | collective-permute-done | bytes 131104 | tf_op jit(solution)/shard_map/ppermute | solution.py:233
  17.2 9.2 %collective-permute-start.9 = (bf16[4,4,16,128]{3,2,1,0:T(8,128)(2,1)S(1)}, bf16[4,4,16,128]{3,2,1,0:T(8,128)(2,1)S(1)}, u32[]{:S(2)}, u32[]{:S(2)}) collective-permute-start(bf16[4,4,16,128]{3,2,1,0:T(8,128)(2,1)S(1)} %pad_maximum_fusion.7), channel_id=1, source_target_pairs={{0,28},{4,24},{8,20},{12,16},{16,12},{20,8},{24,4},{28,0},{1,29},{... | collective-permute-start | bytes 196616 | tf_op jit(solution)/shard_map/ppermute | solution.py:233
  26.4 0.1 collective-permute-start.8
  26.5 0.5 %collective-permute-start.7 = (bf16[4,4,16,128]{3,2,1,0:T(8,128)(2,1)S(1)}, bf16[4,4,16,128]{3,2,1,0:T(8,128)(2,1)S(1)}, u32[]{:S(2)}, u32[]{:S(2)}) collective-permute-start(bf16[4,4,16,128]{3,2,1,0:T(8,128)(2,1)S(1)} %pad_maximum_fusion.5), channel_id=1, source_target_pairs={{0,20},{4,16},{8,28},{12,24},{16,4},{20,0},{24,12},{28,8},{1,21},{... | collective-permute-start | bytes 196616 | tf_op jit(solution)/shard_map/ppermute | solution.py:233
  27.1 0.3 collective-permute-start.6
  27.4 2.3 %collective-permute-start.5 = (bf16[4,4,16,128]{3,2,1,0:T(8,128)(2,1)S(1)}, bf16[4,4,16,128]{3,2,1,0:T(8,128)(2,1)S(1)}, u32[]{:S(2)}, u32[]{:S(2)}) collective-permute-start(bf16[4,4,16,128]{3,2,1,0:T(8,128)(2,1)S(1)} %pad_maximum_fusion.3), channel_id=1, source_target_pairs={{0,12},{4,8},{8,4},{12,0},{16,28},{20,24},{24,20},{28,16},{1,13},{... | collective-permute-start | bytes 196616 | tf_op jit(solution)/shard_map/ppermute | solution.py:233
  29.7 0.2 collective-permute-start.4
  29.9 1.2 %collective-permute-done.8.refs_6_ = bf16[4,4,16,128]{3,2,1,0:T(8,128)(2,1)S(1)} collective-permute-done((bf16[4,4,16,128]{3,2,1,0:T(8,128)(2,1)S(1)}, bf16[4,4,16,128]{3,2,1,0:T(8,128)(2,1)S(1)}, u32[]{:S(2)}, u32[]{:S(2)}) %collective-permute-start.8) | collective-permute-done | bytes 65568 | tf_op jit(solution)/shard_map/ppermute | solution.py:233
  31.2 2.0 %collective-permute-done.5.refs_3_ = bf16[4,4,16,128]{3,2,1,0:T(8,128)(2,1)S(1)} collective-permute-done((bf16[4,4,16,128]{3,2,1,0:T(8,128)(2,1)S(1)}, bf16[4,4,16,128]{3,2,1,0:T(8,128)(2,1)S(1)}, u32[]{:S(2)}, u32[]{:S(2)}) %collective-permute-start.5) | collective-permute-done | bytes 65568 | tf_op jit(solution)/shard_map/ppermute | solution.py:233
  33.2 1.0 %collective-permute-done.4.refs_2_ = bf16[4,4,16,128]{3,2,1,0:T(8,128)(2,1)S(1)} collective-permute-done((bf16[4,4,16,128]{3,2,1,0:T(8,128)(2,1)S(1)}, bf16[4,4,16,128]{3,2,1,0:T(8,128)(2,1)S(1)}, u32[]{:S(2)}, u32[]{:S(2)}) %collective-permute-start.4) | collective-permute-done | bytes 65568 | tf_op jit(solution)/shard_map/ppermute | solution.py:233
  34.2 0.8 %collective-permute-done.3.refs_1_ = bf16[4,4,16,128]{3,2,1,0:T(8,128)(2,1)S(1)} collective-permute-done((bf16[4,4,16,128]{3,2,1,0:T(8,128)(2,1)S(1)}, bf16[4,4,16,128]{3,2,1,0:T(8,128)(2,1)S(1)}, u32[]{:S(2)}, u32[]{:S(2)}) %collective-permute-start.3) | collective-permute-done | bytes 65568 | tf_op jit(solution)/shard_map/ppermute | solution.py:233
  35.0 0.2 gather_early.1.early_ref
  35.2 1.8 %interact.1 = bf16[16,16384]{1,0:T(8,128)(2,1)} custom-call(bf16[16,128,128]{2,1,0:T(8,128)(2,1)S(1)} %gather_early.1.early_ref, bf16[32,4,16,128]{3,2,1,0:T(8,128)(2,1)S(1)} %all-to-all-done.late_ref, bf16[256,256]{1,0:T(8,128)(2,1)S(1)} %convolution_convert_fusion.proj_ref, bf16[1,256]{1,0:T(2,128)(2,1)S(1)} %slice_bitcast_fusion.dense_proj_ref, ...), custom_call_target="tpu_custom_call" | custom-call | tf_op jit(solution)/shard_map/interact/pallas_call | solution.py:214
  (35 shorter events, 0.3 us)
Async XLA Ops:
  3.0 13.2 %copy-start.1 = (bf16[128,257]{0,1:T(8,128)(2,1)S(1)}, bf16[128,257]{0,1:T(8,128)(2,1)}, u32[]{:S(2)}) copy-start(bf16[128,257]{0,1:T(8,128)(2,1)} %param.12) | copy-start | bytes 197380
  3.1 13.3 %copy-start.2 = (bf16[128,257]{0,1:T(8,128)(2,1)S(1)}, bf16[128,257]{0,1:T(8,128)(2,1)}, u32[]{:S(2)}) copy-start(bf16[128,257]{0,1:T(8,128)(2,1)} %param.13) | copy-start | bytes 197380
  3.1 13.3 %copy-start.3 = (s32[256]{0:T(256)S(1)}, s32[256]{0:T(256)}, u32[]{:S(2)}) copy-start(s32[256]{0:T(256)} %param.10) | copy-start | bytes 3076
  3.1 13.6 %collective-permute-start = (bf16[8,4,16,128]{3,2,1,0:T(8,128)(2,1)S(1)}, bf16[8,4,16,128]{3,2,1,0:T(8,128)(2,1)S(1)}, u32[]{:S(2)}, u32[]{:S(2)}) collective-permute-start(bf16[8,4,16,128]{3,2,1,0:T(8,128)(2,1)S(1)} %get-tuple-element.13), channel_id=1, source_target_pairs={{0,1},{1,0},{2,3},{3,2},{4,5},{5,4},{6,7},{7,6},{8,9},{9,8},{10,11... | collective-permute-start | bytes 393224 | tf_op jit(solution)/shard_map/ppermute | solution.py:233
  4.5 12.2 %collective-permute-start.1 = (bf16[8,4,16,128]{3,2,1,0:T(8,128)(2,1)S(1)}, bf16[8,4,16,128]{3,2,1,0:T(8,128)(2,1)S(1)}, u32[]{:S(2)}, u32[]{:S(2)}) collective-permute-start(bf16[8,4,16,128]{3,2,1,0:T(8,128)(2,1)S(1)} %get-tuple-element.14), channel_id=1, source_target_pairs={{0,2},{1,3},{2,0},{3,1},{4,6},{5,7},{6,4},{7,5},{8,10},{9,11},{10,... | collective-permute-start | bytes 393224 | tf_op jit(solution)/shard_map/ppermute | solution.py:233
  4.5 12.6 %collective-permute-start.2 = (bf16[8,4,16,128]{3,2,1,0:T(8,128)(2,1)S(1)}, bf16[8,4,16,128]{3,2,1,0:T(8,128)(2,1)S(1)}, u32[]{:S(2)}, u32[]{:S(2)}) collective-permute-start(bf16[8,4,16,128]{3,2,1,0:T(8,128)(2,1)S(1)} %get-tuple-element.15), channel_id=1, source_target_pairs={{0,3},{1,2},{2,1},{3,0},{4,7},{5,6},{6,5},{7,4},{8,11},{9,10},{10,... | collective-permute-start | bytes 393224 | tf_op jit(solution)/shard_map/ppermute | solution.py:233
  7.8 27.3 %all-to-all-start = ((bf16[32,4,16,128]{3,2,1,0:T(8,128)(2,1)}), bf16[32,4,16,128]{3,2,1,0:T(8,128)(2,1)S(1)}, u32[]{:S(2)}, u32[]{:S(2)}) async-start(bf16[32,4,16,128]{3,2,1,0:T(8,128)(2,1)} %pool_late.1), calls=%async_computation | async-start | bytes 1048576 | tf_op jit(solution)/shard_map/all_to_all | solution.py:240
  15.8 19.3 %copy-start = (bf16[16,128]{1,0:T(8,128)(2,1)S(1)}, bf16[16,128]{1,0:T(8,128)(2,1)}, u32[]{:S(2)}) copy-start(bf16[16,128]{1,0:T(8,128)(2,1)} %dense_ref.1) | copy-start | bytes 12292
  17.2 12.5 %collective-permute-start.9 = (bf16[4,4,16,128]{3,2,1,0:T(8,128)(2,1)S(1)}, bf16[4,4,16,128]{3,2,1,0:T(8,128)(2,1)S(1)}, u32[]{:S(2)}, u32[]{:S(2)}) collective-permute-start(bf16[4,4,16,128]{3,2,1,0:T(8,128)(2,1)S(1)} %pad_maximum_fusion.7), channel_id=1, source_target_pairs={{0,28},{4,24},{8,20},{12,16},{16,12},{20,8},{24,4},{28,0},{1,29},{... | collective-permute-start | bytes 196616 | tf_op jit(solution)/shard_map/ppermute | solution.py:233
  26.4 4.7 %collective-permute-start.8 = (bf16[4,4,16,128]{3,2,1,0:T(8,128)(2,1)S(1)}, bf16[4,4,16,128]{3,2,1,0:T(8,128)(2,1)S(1)}, u32[]{:S(2)}, u32[]{:S(2)}) collective-permute-start(bf16[4,4,16,128]{3,2,1,0:T(8,128)(2,1)S(1)} %pad_maximum_fusion.6), channel_id=1, source_target_pairs={{0,24},{4,28},{8,16},{12,20},{16,8},{20,12},{24,0},{28,4},{1,25},{... | collective-permute-start | bytes 196616 | tf_op jit(solution)/shard_map/ppermute | solution.py:233
  26.5 4.6 %collective-permute-start.7 = (bf16[4,4,16,128]{3,2,1,0:T(8,128)(2,1)S(1)}, bf16[4,4,16,128]{3,2,1,0:T(8,128)(2,1)S(1)}, u32[]{:S(2)}, u32[]{:S(2)}) collective-permute-start(bf16[4,4,16,128]{3,2,1,0:T(8,128)(2,1)S(1)} %pad_maximum_fusion.5), channel_id=1, source_target_pairs={{0,20},{4,16},{8,28},{12,24},{16,4},{20,0},{24,12},{28,8},{1,21},{... | collective-permute-start | bytes 196616 | tf_op jit(solution)/shard_map/ppermute | solution.py:233
  27.1 4.1 %collective-permute-start.6 = (bf16[4,4,16,128]{3,2,1,0:T(8,128)(2,1)S(1)}, bf16[4,4,16,128]{3,2,1,0:T(8,128)(2,1)S(1)}, u32[]{:S(2)}, u32[]{:S(2)}) collective-permute-start(bf16[4,4,16,128]{3,2,1,0:T(8,128)(2,1)S(1)} %pad_maximum_fusion.4), channel_id=1, source_target_pairs={{0,16},{4,20},{8,24},{12,28},{16,0},{20,4},{24,8},{28,12},{1,17},{... | collective-permute-start | bytes 196616 | tf_op jit(solution)/shard_map/ppermute | solution.py:233
  27.4 5.8 %collective-permute-start.5 = (bf16[4,4,16,128]{3,2,1,0:T(8,128)(2,1)S(1)}, bf16[4,4,16,128]{3,2,1,0:T(8,128)(2,1)S(1)}, u32[]{:S(2)}, u32[]{:S(2)}) collective-permute-start(bf16[4,4,16,128]{3,2,1,0:T(8,128)(2,1)S(1)} %pad_maximum_fusion.3), channel_id=1, source_target_pairs={{0,12},{4,8},{8,4},{12,0},{16,28},{20,24},{24,20},{28,16},{1,13},{... | collective-permute-start | bytes 196616 | tf_op jit(solution)/shard_map/ppermute | solution.py:233
  29.7 4.4 %collective-permute-start.4 = (bf16[4,4,16,128]{3,2,1,0:T(8,128)(2,1)S(1)}, bf16[4,4,16,128]{3,2,1,0:T(8,128)(2,1)S(1)}, u32[]{:S(2)}, u32[]{:S(2)}) collective-permute-start(bf16[4,4,16,128]{3,2,1,0:T(8,128)(2,1)S(1)} %pad_maximum_fusion.2), channel_id=1, source_target_pairs={{0,8},{4,12},{8,0},{12,4},{16,24},{20,28},{24,16},{28,20},{1,9},{5... | collective-permute-start | bytes 196616 | tf_op jit(solution)/shard_map/ppermute | solution.py:233
  31.1 3.9 %collective-permute-start.3 = (bf16[4,4,16,128]{3,2,1,0:T(8,128)(2,1)S(1)}, bf16[4,4,16,128]{3,2,1,0:T(8,128)(2,1)S(1)}, u32[]{:S(2)}, u32[]{:S(2)}) collective-permute-start(bf16[4,4,16,128]{3,2,1,0:T(8,128)(2,1)S(1)} %pad_maximum_fusion.1), channel_id=1, source_target_pairs={{0,4},{4,0},{8,12},{12,8},{16,20},{20,16},{24,28},{28,24},{1,5},{5... | collective-permute-start | bytes 196616 | tf_op jit(solution)/shard_map/ppermute | solution.py:233

commit v6 on v5

--- a/solution.py
+++ b/solution.py
@@ -16,7 +16,7 @@
 SAMPLE_BLOCK = 256
 VMEM_LIMIT = 24 * 1024 * 1024
 EARLY = 4
-AHEAD = 1
+AHEAD = 2
 
 
 def count_ids(ids_ref, lens_ref, table, at, block, rows):
@@ -85,8 +85,9 @@
     block, starts = sample_blocks(ids_ref.shape[2])
     rows = table_ref.shape[1]
     ahead = [count_ids(ids_ref, lens_ref, 0, at, block, rows) for at in starts[:AHEAD]]
+    for copy in large:
+        copy.wait()
     for slot in range(early):
-        large[slot].wait()
         for n, at in enumerate(starts):
             counts = ahead[n] if slot == 0 and n < AHEAD else count_ids(ids_ref, lens_ref, slot, at, block, rows)
             pooled = pool_block(table_ref, slot, counts)

time: 37.2 us -> 36.8 us (0.989)
  Pallas kernels: 6.99 us -> 6.51 us
    pallas_call x1, Pallas kernels: 3.04 us -> 2.56 us  [pool_early(): pl.pallas_call(pool_early_kernel, in_specs=[pl.BlockSpec(memory_space=plt...]
where the time goes in v6:
time: 36.8 us; the launch traced here: 36.5 us
  starting transfers between devices  23.3 us (63%)
  Pallas kernels  6.51 us (18%)
  waiting for transfers between devices  5.5 us (15%)
    ppermute x10, starting transfers between devices, swap(): return lax.ppermute(x, axis, [(i, i ^ distance) for i in range(size)])  15.3 us
    all_to_all x1, starting transfers between devices, shards(): late = lax.all_to_all(blocks, AXES, split_axis=0, concat_axis=0, tiled=True)  7.96 us
    ppermute x10, waiting for transfers between devices, swap(): return lax.ppermute(x, axis, [(i, i ^ distance) for i in range(size)])  5.5 us
    pallas_call x1, Pallas kernels, pool_early(): pl.pallas_call(pool_early_kernel, in_specs=[pl.BlockSpec(memory_space=plt...  2.56 us
    pallas_call x1, Pallas kernels, pool_late(): pl.pallas_call(functools.partial(pool_late_kernel, early), in_specs=[pl.B...  2.02 us
    pallas_call x1, Pallas kernels, interact(): pl.pallas_call(interact_kernel, in_specs=[vmem] * 5, out_specs=vmem, out_...  1.77 us
  transfers between devices with their start and end apart: 11, of which 5 were waited for; matrix products, arithmetic and copies ran while one was open for 2% of the time, Pallas kernels for 6%

profile of v6, /device:TPU:17, one launch (start us, length us, event | category | flops | bytes accessed | tf_op | source)
XLA Modules:
  0.0 36.5 jit_solution(9150712077648447840)
XLA Ops:
  0.0 2.6 %pool_early.1 = (bf16[8,4,16,128]{3,2,1,0:T(8,128)(2,1)S(1)}, bf16[8,4,16,128]{3,2,1,0:T(8,128)(2,1)S(1)}, bf16[8,4,16,128]{3,2,1,0:T(8,128)(2,1)S(1)}, bf16[8,4...) custom-call(s32[8,4,512]{2,1,0:T(4,128)} %bitcast.3, ...), custom_call_target="tpu_custom_call" | custom-call | flops 536870912 | bytes 1572864 | tf_op jit(solution)/shard_map/pool_early/pallas_call | solution.py:107
  2.6 1.4 %collective-permute-start = (bf16[8,4,16,128]{3,2,1,0:T(8,128)(2,1)S(1)}, bf16[8,4,16,128]{3,2,1,0:T(8,128)(2,1)S(1)}, u32[]{:S(2)}, u32[]{:S(2)}) collective-permute-start(bf16[8,4,16,128]{3,2,1,0:T(8,128)(2,1)S(1)} %get-tuple-element.13), channel_id=1, source_target_pairs={{0,1},{1,0},{2,3},{3,2},{4,5},{5,4},{6,7},{7,6},{8,9},{9,8},{10,11... | collective-permute-start | bytes 393224 | tf_op jit(solution)/shard_map/ppermute | solution.py:234
  4.0 0.1 collective-permute-start.1
  4.0 1.3 %collective-permute-start.2 = (bf16[8,4,16,128]{3,2,1,0:T(8,128)(2,1)S(1)}, bf16[8,4,16,128]{3,2,1,0:T(8,128)(2,1)S(1)}, u32[]{:S(2)}, u32[]{:S(2)}) collective-permute-start(bf16[8,4,16,128]{3,2,1,0:T(8,128)(2,1)S(1)} %get-tuple-element.15), channel_id=1, source_target_pairs={{0,3},{1,2},{2,1},{3,0},{4,7},{5,6},{6,5},{7,4},{8,11},{9,10},{10,... | collective-permute-start | bytes 393224 | tf_op jit(solution)/shard_map/ppermute | solution.py:234
  5.3 2.0 %pool_late.1 = bf16[32,4,16,128]{3,2,1,0:T(8,128)(2,1)} custom-call(s32[8,4,512]{2,1,0:T(4,128)S(1)} %get-tuple-element.16.ids_ref, s32[8,512]{1,0:T(8,128)S(1)} %get-tuple-element.17.lens_ref, bf16[4,1024,128]{2,1,0:T(8,128)(2,1)S(1)} %get-tuple-element.18.table_ref), custom_call_target="tpu_custom_call" | custom-call | flops 536870912 | bytes 1572864 | tf_op jit(solution)/shard_map/pool_late/pallas_call | solution.py:143
  7.3 8.0 %all-to-all-start = ((bf16[32,4,16,128]{3,2,1,0:T(8,128)(2,1)}), bf16[32,4,16,128]{3,2,1,0:T(8,128)(2,1)S(1)}, u32[]{:S(2)}, u32[]{:S(2)}) async-start(bf16[32,4,16,128]{3,2,1,0:T(8,128)(2,1)} %pool_late.1), calls=%async_computation | async-start | bytes 1048576 | tf_op jit(solution)/shard_map/all_to_all | solution.py:241
  15.4 0.1 iota_add_fusion
  15.5 0.1 add.28
  15.6 0.1 broadcast_add_fusion
  15.7 0.1 add.31
  15.9 0.3 convolution_convert_fusion.proj_ref
  16.2 0.4 %collective-permute-done.2 = bf16[8,4,16,128]{3,2,1,0:T(8,128)(2,1)S(1)} collective-permute-done((bf16[8,4,16,128]{3,2,1,0:T(8,128)(2,1)S(1)}, bf16[8,4,16,128]{3,2,1,0:T(8,128)(2,1)S(1)}, u32[]{:S(2)}, u32[]{:S(2)}) %collective-permute-start.2) | collective-permute-done | bytes 131104 | tf_op jit(solution)/shard_map/ppermute | solution.py:234
  16.7 9.2 %collective-permute-start.9 = (bf16[4,4,16,128]{3,2,1,0:T(8,128)(2,1)S(1)}, bf16[4,4,16,128]{3,2,1,0:T(8,128)(2,1)S(1)}, u32[]{:S(2)}, u32[]{:S(2)}) collective-permute-start(bf16[4,4,16,128]{3,2,1,0:T(8,128)(2,1)S(1)} %pad_maximum_fusion.7), channel_id=1, source_target_pairs={{0,28},{4,24},{8,20},{12,16},{16,12},{20,8},{24,4},{28,0},{1,29},{... | collective-permute-start | bytes 196616 | tf_op jit(solution)/shard_map/ppermute | solution.py:234
  26.0 0.1 collective-permute-start.8
  26.1 0.6 %collective-permute-start.7 = (bf16[4,4,16,128]{3,2,1,0:T(8,128)(2,1)S(1)}, bf16[4,4,16,128]{3,2,1,0:T(8,128)(2,1)S(1)}, u32[]{:S(2)}, u32[]{:S(2)}) collective-permute-start(bf16[4,4,16,128]{3,2,1,0:T(8,128)(2,1)S(1)} %pad_maximum_fusion.5), channel_id=1, source_target_pairs={{0,20},{4,16},{8,28},{12,24},{16,4},{20,0},{24,12},{28,8},{1,21},{... | collective-permute-start | bytes 196616 | tf_op jit(solution)/shard_map/ppermute | solution.py:234
  26.6 0.3 collective-permute-start.6
  26.9 2.3 %collective-permute-start.5 = (bf16[4,4,16,128]{3,2,1,0:T(8,128)(2,1)S(1)}, bf16[4,4,16,128]{3,2,1,0:T(8,128)(2,1)S(1)}, u32[]{:S(2)}, u32[]{:S(2)}) collective-permute-start(bf16[4,4,16,128]{3,2,1,0:T(8,128)(2,1)S(1)} %pad_maximum_fusion.3), channel_id=1, source_target_pairs={{0,12},{4,8},{8,4},{12,0},{16,28},{20,24},{24,20},{28,16},{1,13},{... | collective-permute-start | bytes 196616 | tf_op jit(solution)/shard_map/ppermute | solution.py:234
  29.3 0.2 collective-permute-start.4
  29.4 1.2 %collective-permute-done.8.refs_6_ = bf16[4,4,16,128]{3,2,1,0:T(8,128)(2,1)S(1)} collective-permute-done((bf16[4,4,16,128]{3,2,1,0:T(8,128)(2,1)S(1)}, bf16[4,4,16,128]{3,2,1,0:T(8,128)(2,1)S(1)}, u32[]{:S(2)}, u32[]{:S(2)}) %collective-permute-start.8) | collective-permute-done | bytes 65568 | tf_op jit(solution)/shard_map/ppermute | solution.py:234
  30.7 2.0 %collective-permute-done.5.refs_3_ = bf16[4,4,16,128]{3,2,1,0:T(8,128)(2,1)S(1)} collective-permute-done((bf16[4,4,16,128]{3,2,1,0:T(8,128)(2,1)S(1)}, bf16[4,4,16,128]{3,2,1,0:T(8,128)(2,1)S(1)}, u32[]{:S(2)}, u32[]{:S(2)}) %collective-permute-start.5) | collective-permute-done | bytes 65568 | tf_op jit(solution)/shard_map/ppermute | solution.py:234
  32.8 1.0 %collective-permute-done.4.refs_2_ = bf16[4,4,16,128]{3,2,1,0:T(8,128)(2,1)S(1)} collective-permute-done((bf16[4,4,16,128]{3,2,1,0:T(8,128)(2,1)S(1)}, bf16[4,4,16,128]{3,2,1,0:T(8,128)(2,1)S(1)}, u32[]{:S(2)}, u32[]{:S(2)}) %collective-permute-start.4) | collective-permute-done | bytes 65568 | tf_op jit(solution)/shard_map/ppermute | solution.py:234
  33.7 0.8 %collective-permute-done.3.refs_1_ = bf16[4,4,16,128]{3,2,1,0:T(8,128)(2,1)S(1)} collective-permute-done((bf16[4,4,16,128]{3,2,1,0:T(8,128)(2,1)S(1)}, bf16[4,4,16,128]{3,2,1,0:T(8,128)(2,1)S(1)}, u32[]{:S(2)}, u32[]{:S(2)}) %collective-permute-start.3) | collective-permute-done | bytes 65568 | tf_op jit(solution)/shard_map/ppermute | solution.py:234
  34.5 0.2 gather_early.1.early_ref
  34.7 1.8 %interact.1 = bf16[16,16384]{1,0:T(8,128)(2,1)} custom-call(bf16[16,128,128]{2,1,0:T(8,128)(2,1)S(1)} %gather_early.1.early_ref, bf16[32,4,16,128]{3,2,1,0:T(8,128)(2,1)S(1)} %all-to-all-done.late_ref, bf16[256,256]{1,0:T(8,128)(2,1)S(1)} %convolution_convert_fusion.proj_ref, bf16[1,256]{1,0:T(2,128)(2,1)S(1)} %slice_bitcast_fusion.dense_proj_ref, ...), custom_call_target="tpu_custom_call" | custom-call | tf_op jit(solution)/shard_map/interact/pallas_call | solution.py:215
  (35 shorter events, 0.3 us)
Async XLA Ops:
  2.6 13.2 %copy-start.1 = (bf16[128,257]{0,1:T(8,128)(2,1)S(1)}, bf16[128,257]{0,1:T(8,128)(2,1)}, u32[]{:S(2)}) copy-start(bf16[128,257]{0,1:T(8,128)(2,1)} %param.12) | copy-start | bytes 197380
  2.6 13.3 %copy-start.2 = (bf16[128,257]{0,1:T(8,128)(2,1)S(1)}, bf16[128,257]{0,1:T(8,128)(2,1)}, u32[]{:S(2)}) copy-start(bf16[128,257]{0,1:T(8,128)(2,1)} %param.13) | copy-start | bytes 197380
  2.6 13.3 %copy-start.3 = (s32[256]{0:T(256)S(1)}, s32[256]{0:T(256)}, u32[]{:S(2)}) copy-start(s32[256]{0:T(256)} %param.10) | copy-start | bytes 3076
  2.6 13.6 %collective-permute-start = (bf16[8,4,16,128]{3,2,1,0:T(8,128)(2,1)S(1)}, bf16[8,4,16,128]{3,2,1,0:T(8,128)(2,1)S(1)}, u32[]{:S(2)}, u32[]{:S(2)}) collective-permute-start(bf16[8,4,16,128]{3,2,1,0:T(8,128)(2,1)S(1)} %get-tuple-element.13), channel_id=1, source_target_pairs={{0,1},{1,0},{2,3},{3,2},{4,5},{5,4},{6,7},{7,6},{8,9},{9,8},{10,11... | collective-permute-start | bytes 393224 | tf_op jit(solution)/shard_map/ppermute | solution.py:234
  4.0 12.2 %collective-permute-start.1 = (bf16[8,4,16,128]{3,2,1,0:T(8,128)(2,1)S(1)}, bf16[8,4,16,128]{3,2,1,0:T(8,128)(2,1)S(1)}, u32[]{:S(2)}, u32[]{:S(2)}) collective-permute-start(bf16[8,4,16,128]{3,2,1,0:T(8,128)(2,1)S(1)} %get-tuple-element.14), channel_id=1, source_target_pairs={{0,2},{1,3},{2,0},{3,1},{4,6},{5,7},{6,4},{7,5},{8,10},{9,11},{10,... | collective-permute-start | bytes 393224 | tf_op jit(solution)/shard_map/ppermute | solution.py:234
  4.0 12.7 %collective-permute-start.2 = (bf16[8,4,16,128]{3,2,1,0:T(8,128)(2,1)S(1)}, bf16[8,4,16,128]{3,2,1,0:T(8,128)(2,1)S(1)}, u32[]{:S(2)}, u32[]{:S(2)}) collective-permute-start(bf16[8,4,16,128]{3,2,1,0:T(8,128)(2,1)S(1)} %get-tuple-element.15), channel_id=1, source_target_pairs={{0,3},{1,2},{2,1},{3,0},{4,7},{5,6},{6,5},{7,4},{8,11},{9,10},{10,... | collective-permute-start | bytes 393224 | tf_op jit(solution)/shard_map/ppermute | solution.py:234
  7.3 27.3 %all-to-all-start = ((bf16[32,4,16,128]{3,2,1,0:T(8,128)(2,1)}), bf16[32,4,16,128]{3,2,1,0:T(8,128)(2,1)S(1)}, u32[]{:S(2)}, u32[]{:S(2)}) async-start(bf16[32,4,16,128]{3,2,1,0:T(8,128)(2,1)} %pool_late.1), calls=%async_computation | async-start | bytes 1048576 | tf_op jit(solution)/shard_map/all_to_all | solution.py:241
  15.3 19.4 %copy-start = (bf16[16,128]{1,0:T(8,128)(2,1)S(1)}, bf16[16,128]{1,0:T(8,128)(2,1)}, u32[]{:S(2)}) copy-start(bf16[16,128]{1,0:T(8,128)(2,1)} %dense_ref.1) | copy-start | bytes 12292
  16.7 12.5 %collective-permute-start.9 = (bf16[4,4,16,128]{3,2,1,0:T(8,128)(2,1)S(1)}, bf16[4,4,16,128]{3,2,1,0:T(8,128)(2,1)S(1)}, u32[]{:S(2)}, u32[]{:S(2)}) collective-permute-start(bf16[4,4,16,128]{3,2,1,0:T(8,128)(2,1)S(1)} %pad_maximum_fusion.7), channel_id=1, source_target_pairs={{0,28},{4,24},{8,20},{12,16},{16,12},{20,8},{24,4},{28,0},{1,29},{... | collective-permute-start | bytes 196616 | tf_op jit(solution)/shard_map/ppermute | solution.py:234
  26.0 4.7 %collective-permute-start.8 = (bf16[4,4,16,128]{3,2,1,0:T(8,128)(2,1)S(1)}, bf16[4,4,16,128]{3,2,1,0:T(8,128)(2,1)S(1)}, u32[]{:S(2)}, u32[]{:S(2)}) collective-permute-start(bf16[4,4,16,128]{3,2,1,0:T(8,128)(2,1)S(1)} %pad_maximum_fusion.6), channel_id=1, source_target_pairs={{0,24},{4,28},{8,16},{12,20},{16,8},{20,12},{24,0},{28,4},{1,25},{... | collective-permute-start | bytes 196616 | tf_op jit(solution)/shard_map/ppermute | solution.py:234
  26.1 4.6 %collective-permute-start.7 = (bf16[4,4,16,128]{3,2,1,0:T(8,128)(2,1)S(1)}, bf16[4,4,16,128]{3,2,1,0:T(8,128)(2,1)S(1)}, u32[]{:S(2)}, u32[]{:S(2)}) collective-permute-start(bf16[4,4,16,128]{3,2,1,0:T(8,128)(2,1)S(1)} %pad_maximum_fusion.5), channel_id=1, source_target_pairs={{0,20},{4,16},{8,28},{12,24},{16,4},{20,0},{24,12},{28,8},{1,21},{... | collective-permute-start | bytes 196616 | tf_op jit(solution)/shard_map/ppermute | solution.py:234
  26.6 4.1 %collective-permute-start.6 = (bf16[4,4,16,128]{3,2,1,0:T(8,128)(2,1)S(1)}, bf16[4,4,16,128]{3,2,1,0:T(8,128)(2,1)S(1)}, u32[]{:S(2)}, u32[]{:S(2)}) collective-permute-start(bf16[4,4,16,128]{3,2,1,0:T(8,128)(2,1)S(1)} %pad_maximum_fusion.4), channel_id=1, source_target_pairs={{0,16},{4,20},{8,24},{12,28},{16,0},{20,4},{24,8},{28,12},{1,17},{... | collective-permute-start | bytes 196616 | tf_op jit(solution)/shard_map/ppermute | solution.py:234
  26.9 5.9 %collective-permute-start.5 = (bf16[4,4,16,128]{3,2,1,0:T(8,128)(2,1)S(1)}, bf16[4,4,16,128]{3,2,1,0:T(8,128)(2,1)S(1)}, u32[]{:S(2)}, u32[]{:S(2)}) collective-permute-start(bf16[4,4,16,128]{3,2,1,0:T(8,128)(2,1)S(1)} %pad_maximum_fusion.3), channel_id=1, source_target_pairs={{0,12},{4,8},{8,4},{12,0},{16,28},{20,24},{24,20},{28,16},{1,13},{... | collective-permute-start | bytes 196616 | tf_op jit(solution)/shard_map/ppermute | solution.py:234
  29.3 4.5 %collective-permute-start.4 = (bf16[4,4,16,128]{3,2,1,0:T(8,128)(2,1)S(1)}, bf16[4,4,16,128]{3,2,1,0:T(8,128)(2,1)S(1)}, u32[]{:S(2)}, u32[]{:S(2)}) collective-permute-start(bf16[4,4,16,128]{3,2,1,0:T(8,128)(2,1)S(1)} %pad_maximum_fusion.2), channel_id=1, source_target_pairs={{0,8},{4,12},{8,0},{12,4},{16,24},{20,28},{24,16},{28,20},{1,9},{5... | collective-permute-start | bytes 196616 | tf_op jit(solution)/shard_map/ppermute | solution.py:234
  30.7 3.9 %collective-permute-start.3 = (bf16[4,4,16,128]{3,2,1,0:T(8,128)(2,1)S(1)}, bf16[4,4,16,128]{3,2,1,0:T(8,128)(2,1)S(1)}, u32[]{:S(2)}, u32[]{:S(2)}) collective-permute-start(bf16[4,4,16,128]{3,2,1,0:T(8,128)(2,1)S(1)} %pad_maximum_fusion.1), channel_id=1, source_target_pairs={{0,4},{4,0},{8,12},{12,8},{16,20},{20,16},{24,28},{28,24},{1,5},{5... | collective-permute-start | bytes 196616 | tf_op jit(solution)/shard_map/ppermute | solution.py:234
